TPU v7x, 256 devices: a whole 4x4x8 slice. The times are simulated.
256 devices in a mesh: row: 8 (over x, core), col: 32 (over y, z).
Axes of the slice: x: 4, y: 4, z: 8, core: 2. Of those that a mesh axis runs over, the one named last changes fastest.
Arguments:
- kernel: float32 [16384, 16384], P('row', 'col'), as said below
Outputs:
- factored: float32 [16384, 16384], P('row', 'col')
Inputs may be any that keep to these rules, and one draw needn't show every extreme that they name: `kernel`: in logical order the matrix is symmetric and positive definite, with smallest eigenvalue 0.3 or more.
All inputs are finite; a program needn't handle non-finite values.
Results may differ from a plain program's by a relative error of at most 0.0003.
Values sent between devices are 32-bit elements; how exact they have to be, the bound alone decides.
A program may use at most 64 MiB of HBM per device.

v0:
```python
import jax
import jax.numpy as jnp
from jax import lax
from jax.sharding import PartitionSpec as P

NB = 256


def from_root(shard, axis, root):
    mine = lax.axis_index(axis) == root
    return lax.psum(jnp.where(mine, shard, jnp.zeros_like(shard)), axis)


def product(first_op, second_op):
    return lax.dot_general(
        first_op,
        second_op,
        (((1,), (1,)), ((), ())),
        precision=lax.Precision.HIGHEST,
        preferred_element_type=jnp.float32,
    )


def solve_panel(factor_low, row_data):
    return jax.scipy.linalg.solve_triangular(factor_low, row_data.T, lower=True).T


def pick_blocks(row_data, column, grid_rows, stride_blocks):
    panel_width = row_data.shape[1]
    shaped = row_data.reshape(
        row_data.shape[0] // (stride_blocks * NB), stride_blocks, NB, panel_width
    )
    chosen = lax.dynamic_index_in_dim(shaped, column // grid_rows, 1, keepdims=False)
    return chosen.reshape(-1, panel_width)


def factor_panel(panel_raw, panel_index, grid_rows, grid_cols, column):
    stride_blocks = grid_cols // grid_rows
    own_row = panel_index % grid_rows
    own_col = panel_index % grid_cols
    start_row = panel_index // grid_rows * NB
    diag_raw = jnp.where(
        column == own_col, panel_raw[start_row : start_row + NB], jnp.eye(NB, dtype=jnp.float32)
    )
    diagonal = from_root(diag_raw, "row", own_row)
    factor_low = jnp.linalg.cholesky(diagonal)
    solved_rows = solve_panel(factor_low, panel_raw)
    rows_out = from_root(solved_rows, "col", own_col)
    cols_out = from_root(
        pick_blocks(rows_out, column, grid_rows, stride_blocks), "row", column % grid_rows
    )
    return (factor_low, rows_out, cols_out)


def local(kernel):
    grid_rows = lax.axis_size("row")
    grid_cols = lax.axis_size("col")
    my_row = lax.axis_index("row")
    my_col = lax.axis_index("col")
    local_rows = kernel.shape[0]
    local_cols = kernel.shape[1]
    row_iota = jnp.arange(local_rows, dtype=jnp.int32)
    col_iota = jnp.arange(local_cols, dtype=jnp.int32)
    row_block = row_iota // NB * grid_rows + my_row
    col_block = col_iota // NB * grid_cols + my_col

    def masked(panel_index, rows_in, cols_in):
        return (
            jnp.where(row_block[:, None] > panel_index, rows_in, 0.0),
            jnp.where(col_block[:, None] > panel_index, cols_in, 0.0),
        )

    def settle(section, col_lo, panel_index, factor_low, rows_in):
        own_row = panel_index % grid_rows
        own_col = panel_index % grid_cols
        start_row = panel_index // grid_rows * NB
        start_col = panel_index // grid_cols * NB - col_lo
        tiled_low = jnp.tile(factor_low, (local_rows // NB, 1))
        block_ids = row_block[:, None]
        new_block = jnp.where(
            block_ids > panel_index, rows_in, jnp.where(block_ids == panel_index, tiled_low, 0.0)
        )
        old_block = section[:, start_col : start_col + NB]
        section = section.at[:, start_col : start_col + NB].set(
            jnp.where(my_col == own_col, new_block, old_block)
        )
        col_ids = col_block[None, col_lo : col_lo + section.shape[1]]
        cleared = jnp.where(
            (my_row == own_row) & (col_ids > panel_index), 0.0, section[start_row : start_row + NB]
        )
        return section.at[start_row : start_row + NB].set(cleared)

    matrix = kernel
    factor_one, rows_one, cols_one = factor_panel(matrix[:, :NB], 0, grid_rows, grid_cols, my_col)
    used_rows, used_cols = masked(0, rows_one, cols_one)
    matrix = settle(matrix - product(used_rows, used_cols), 0, 0, factor_one, rows_one)
    factor_two, rows_two, cols_two = factor_panel(matrix[:, :NB], 1, grid_rows, grid_cols, my_col)
    used_rows, used_cols = masked(1, rows_two, cols_two)
    matrix = settle(matrix - product(used_rows, used_cols), 0, 1, factor_two, rows_two)
    return matrix


def solution(mesh):
    placed = (P("row", "col"),)
    return jax.shard_map(
        local, mesh=mesh, in_specs=placed, out_specs=P("row", "col"), check_vma=False
    )
```

profile of v0, /device:TPU:103, one launch (start us, length us, event | category | flops | bytes accessed | tf_op | source)
XLA Modules:
  0.0 770.8 jit_solution(12734155929222158375)
XLA Ops:
  6.5 5.3 copy.4
  11.9 1.7 fusion.19
  13.6 1.7 slice_bitcast_fusion.1
  15.4 63.7 %all-reduce.8.cloned.1.call-done = f32[256,256]{0,1:T(8,128)} async-done(((f32[256,256]{0,1:T(8,128)}), f32[256,256]{0,1:T(8,128)}) %all-reduce.8.cloned.1.call-update) | async-done | bytes 262160 | tf_op jit(solution)/shard_map/psum | solution.py:11
  79.1 1.1 copy.3
  80.2 1.0 fusion.22
  81.2 11.7 %cholesky.130 = f32[128,128]{1,0:T(8,128)S(1)} custom-call(f32[128,128]{1,0:T(8,128)S(1)} %cholesky.194), custom_call_target="Cholesky" | custom-call | tf_op jit(solution)/shard_map/jit(cholesky)/cholesky | solution.py:46
  92.9 9.8 %custom-call.13 = f32[1,128,128]{1,2,0:T(8,128)S(1)} custom-call(f32[1,128,128]{2,1,0:T(8,128)S(1)} %get-tuple-element.104), custom_call_target="InvertDiagBlocksLowerTriangular" | custom-call | tf_op jit(solution)/shard_map/jit(cholesky)/cholesky | solution.py:46
  103.0 0.3 convolution_subtract_fusion.5
  103.2 11.7 %cholesky.147 = f32[128,128]{1,0:T(8,128)S(1)} custom-call(f32[128,128]{1,0:T(8,128)S(1)} %convolution_subtract_fusion.5), custom_call_target="Cholesky" | custom-call | tf_op jit(solution)/shard_map/jit(cholesky)/cholesky | solution.py:46
  115.0 0.7 compare_reduce_fusion.2
  117.1 13.8 %while.8 = (s32[]{:T(128)}, f32[256,256]{1,0:T(8,128)S(1)}, s32[2,2]{1,0:T(2,128)S(1)}, f32[2,128,128]{2,1,0:T(8,128)S(1)}, s32[]{:T(128)}) while((s32[]{:T(128)}, f32[256,256]{1,0:T(8,128)S(1)}, s32[2,2]{1,0:T(2,128)S(1)}, f32[2,128,128]{2,1,0:T(8,128)S(1)}, s32[]{:T(128)}) %tuple.66), condition=%wide.while_cond.4, body=%wide.while_body.4.sunk | while | flops 2 | bytes 131181 | solution.py:25
  126.8 0.7 fusion.69
  127.5 1.3 bitcast_dynamic-update-slice_fusion.4
  128.9 0.7 fusion.69
  129.5 1.3 bitcast_dynamic-update-slice_fusion.4
  130.9 19.7 %custom-call.14 = f32[2,128,128]{1,2,0:T(8,128)S(1)} custom-call(f32[2,128,128]{2,1,0:T(8,128)S(1)} %get-tuple-element.69), custom_call_target="InvertDiagBlocksLowerTriangular" | custom-call | tf_op jit(solution)/shard_map/jit(_solve_triangular)/triangular_solve | solution.py:25
  150.6 1.1 fusion.8
  151.6 1.8 convolution_subtract_fusion.3
  153.5 1.1 fusion.35
  154.5 1.4 fusion.2
  156.1 148.8 %all-reduce.10.cloned.1.call-done = f32[2048,256]{0,1:T(8,128)} async-done(((f32[2048,256]{0,1:T(8,128)}), f32[2048,256]{0,1:T(8,128)}) %all-reduce.10.cloned.1.call-update) | async-done | bytes 2097168 | tf_op jit(solution)/shard_map/psum | solution.py:11
  304.9 2.7 reshape.209
  307.6 1.8 fusion.14
  309.4 0.9 copy.13
  310.3 0.7 compare_reduce_fusion.4
  311.3 2.2 copy.14
  313.5 64.3 %all-reduce.12.cloned.1.call-done = f32[512,256]{0,1:T(8,128)} async-done(((f32[512,256]{0,1:T(8,128)}), f32[512,256]{0,1:T(8,128)}) %all-reduce.12.cloned.1.call-update) | async-done | bytes 524304 | tf_op jit(solution)/shard_map/psum | solution.py:11
  377.8 7.0 convolution_subtract_fusion.1
  384.8 4.2 fusion
  389.0 2.0 constant_dynamic-update-slice_fusion.2
  391.0 0.7 fusion.20
  391.7 0.4 all-reduce.16.cloned.1.call-start
  392.2 1.7 slice_bitcast_fusion
  393.9 62.0 %all-reduce.14.cloned.1.call-done = f32[256,256]{0,1:T(8,128)} async-done(((f32[256,256]{0,1:T(8,128)}), f32[256,256]{0,1:T(8,128)}) %all-reduce.14.cloned.1.call-update) | async-done | bytes 262160 | tf_op jit(solution)/shard_map/psum | solution.py:11
  455.9 1.1 copy.7
  457.0 1.0 fusion.21
  458.0 11.7 %cholesky.164 = f32[128,128]{1,0:T(8,128)S(1)} custom-call(f32[128,128]{1,0:T(8,128)S(1)} %cholesky.197), custom_call_target="Cholesky" | custom-call | tf_op jit(solution)/shard_map/jit(cholesky)/cholesky | solution.py:46
  469.8 9.8 %custom-call.15 = f32[1,128,128]{1,2,0:T(8,128)S(1)} custom-call(f32[1,128,128]{2,1,0:T(8,128)S(1)} %get-tuple-element.100), custom_call_target="InvertDiagBlocksLowerTriangular" | custom-call | tf_op jit(solution)/shard_map/jit(cholesky)/cholesky | solution.py:46
  479.6 0.2 constant_dynamic-update-slice_fusion
  479.8 0.3 convolution_subtract_fusion.4
  480.1 11.7 %cholesky.181 = f32[128,128]{1,0:T(8,128)S(1)} custom-call(f32[128,128]{1,0:T(8,128)S(1)} %convolution_subtract_fusion.4), custom_call_target="Cholesky" | custom-call | tf_op jit(solution)/shard_map/jit(cholesky)/cholesky | solution.py:46
  491.8 0.7 compare_reduce_fusion
  492.6 0.7 compare_reduce_fusion.1
  494.7 4.4 while.9
  494.9 0.7 fusion.70
  495.5 1.4 bitcast_dynamic-update-slice_fusion.5
  497.0 0.7 fusion.70
  497.6 1.4 bitcast_dynamic-update-slice_fusion.5
  499.0 19.7 %custom-call.16 = f32[2,128,128]{1,2,0:T(8,128)S(1)} custom-call(f32[2,128,128]{2,1,0:T(8,128)S(1)} %get-tuple-element.70), custom_call_target="InvertDiagBlocksLowerTriangular" | custom-call | tf_op jit(solution)/shard_map/jit(_solve_triangular)/triangular_solve | solution.py:25
  518.7 1.0 fusion.6
  519.8 1.0 convolution_subtract_fusion.2
  520.8 1.1 fusion.31
  521.9 1.4 fusion.3
  523.4 148.9 %all-reduce.16.cloned.1.call-done = f32[2048,256]{0,1:T(8,128)} async-done(((f32[2048,256]{0,1:T(8,128)}), f32[2048,256]{0,1:T(8,128)}) %all-reduce.16.cloned.1.call-update) | async-done | bytes 2097168 | tf_op jit(solution)/shard_map/psum | solution.py:11
  672.2 2.7 reshape.210
  674.9 1.8 fusion.15
  676.7 0.8 copy.15
  677.9 2.2 copy.16
  680.1 65.0 %all-reduce.18.cloned.1.call-done = f32[512,256]{0,1:T(8,128)} async-done(((f32[512,256]{0,1:T(8,128)}), f32[512,256]{0,1:T(8,128)}) %all-reduce.18.cloned.1.call-update) | async-done | bytes 524304 | tf_op jit(solution)/shard_map/psum | solution.py:11
  745.2 7.0 convolution_subtract_fusion
  752.2 4.2 fusion.1
  756.4 2.0 fusion.16
  758.4 5.3 copy.10
  (46 shorter events, 1.4 us)
Async XLA Ops:
  6.5 72.6 %all-reduce.8.cloned.1.call-start = ((), (), s32[]{:S(2)}) async-start(), calls=%async_computation | async-start | bytes 524288 | tf_op jit(solution)/shard_map/psum | solution.py:11
  13.6 291.3 %all-reduce.10.cloned.1.call-start = ((), (), s32[]{:S(2)}) async-start(), calls=%async_computation.1 | async-start | bytes 4194304 | tf_op jit(solution)/shard_map/psum | solution.py:11
  156.0 221.8 %all-reduce.12.cloned.1.call-start = ((), (), s32[]{:S(2)}) async-start(), calls=%async_computation.2 | async-start | bytes 1048576 | tf_op jit(solution)/shard_map/psum | solution.py:11
  310.2 145.7 %all-reduce.14.cloned.1.call-start = ((), (), s32[]{:S(2)}) async-start(), calls=%async_computation.3 | async-start | bytes 524288 | tf_op jit(solution)/shard_map/psum | solution.py:11
  311.3 66.5 %copy-start = (f32[2048,256]{0,1:T(8,128)S(1)}, f32[2048,256]{0,1:T(8,128)}, u32[]{:S(2)}) copy-start(f32[2048,256]{0,1:T(8,128)} %all-reduce.10.cloned.1.call-done) | copy-start | bytes 6291460
  377.8 7.0 copy-start.3
  391.7 280.5 %all-reduce.16.cloned.1.call-start = ((), (), s32[]{:S(2)}) async-start(), calls=%async_computation.4 | async-start | bytes 4194304 | tf_op jit(solution)/shard_map/psum | solution.py:11
  523.3 221.8 %all-reduce.18.cloned.1.call-start = ((), (), s32[]{:S(2)}) async-start(), calls=%async_computation.5 | async-start | bytes 1048576 | tf_op jit(solution)/shard_map/psum | solution.py:11
  677.9 67.2 %copy-start.1 = (f32[2048,256]{0,1:T(8,128)S(1)}, f32[2048,256]{0,1:T(8,128)}, u32[]{:S(2)}) copy-start(f32[2048,256]{0,1:T(8,128)} %all-reduce.16.cloned.1.call-done) | copy-start | bytes 6291460
  745.1 7.0 copy-start.2
Sparse Core Ops, SparseCore 0:
  13.7 65.3 all-reduce.7
  156.1 148.7 all-reduce.9
  310.4 67.3 all-reduce.11
  391.9 64.0 all-reduce.13
  523.4 148.7 all-reduce.15
  677.7 67.3 all-reduce.17
where the time goes:
time: 782 us; the launch traced here: 771 us
  waiting for transfers between devices  553 us (71%)
  other arithmetic  132 us (17%)
  local copies, waits for them, and re-layouts  36.6 us (5%)
  matrix products  22.1 us (3%)
  between operations  16.6 us (2%)
  loops' own time  9.96 us (1%)
    psum x6, waiting for transfers between devices, from_root(): return lax.psum(jnp.where(mine, shard, jnp.zeros_like(shard)), axis)  553 us
    another operation x13, other arithmetic, factor_panel(): factor_low = jnp.linalg.cholesky(diagonal)  68.8 us
    another operation x5, other arithmetic, solve_panel(): jax.scipy.linalg.solve_triangular(factor_low, row_data.T, lower=True)  39.4 us
  transfers between devices with their start and end apart: 6, of which 6 were waited for; matrix products, arithmetic and copies ran while one was open for 1% of the time, Pallas kernels for 0%

commit v1 on v0

v1 whole, which is shorter than its diff:
```python
import jax
import jax.numpy as jnp
from jax import lax
from jax.experimental import pallas as pl
from jax.experimental.pallas import tpu as pltpu
from jax.sharding import PartitionSpec as P

NB = 256
F32 = jnp.float32
MESH = pl.DeviceIdType.MESH
HI = lax.Precision.HIGHEST

CH = 64
PC_N = 512 // CH
D_N = NB // CH
R_N = 2 * PC_N
LAG = 2
ZP, ZM, YP, YM, XP, XM, PA = range(7)


def dot(a, b, ca=1, cb=0):
    return lax.dot_general(
        a, b, (((ca,), (cb,)), ((), ())), precision=HI, preferred_element_type=F32
    )


def comm_kernel(
    a, pc, rr, dd, head, headt, dsend, drecv, psend, precv, zsend, zrecv, ysend, yrecv, lsem
):
    row = lax.axis_index("row")
    col = lax.axis_index("col")
    x, k = row // 2, row % 2
    y, z = col // 8, col % 8

    def at(nx, ny, nz, nk):
        return ((nx % 4) * 2 + nk, (ny % 4) * 8 + nz % 8)

    near = {
        ZP: at(x, y, z + 1, k),
        ZM: at(x, y, z + 7, k),
        YP: at(x, y + 1, z, k),
        YM: at(x, y + 3, z, k),
        XP: at(x + 1, y, z, k),
        XM: at(x + 3, y, z, k),
        PA: at(x, y, z, 1 - k),
    }
    barrier = pltpu.get_barrier_semaphore()
    for target in near.values():
        pl.semaphore_signal(barrier, inc=1, device_id=target, device_id_type=MESH)

    def remote(src, dst, send, recv, way):
        return pltpu.make_async_remote_copy(
            src_ref=src, dst_ref=dst, send_sem=send, recv_sem=recv,
            device_id=near[way], device_id_type=MESH,
        )

    load = pltpu.make_async_copy(a.at[pl.ds(0, NB), :], head, lsem.at[0])
    load.start()
    load.wait()
    headt[...] = head[...].T
    fill = pltpu.make_async_copy(headt, pc.at[k], lsem.at[1])

    @pl.when(x == 0)
    def _():
        fill.start()
        fill.wait()

    roots = ((0, 0), (0, 1), (1, 1))
    for i, (dk, dz0) in enumerate(roots):
        @pl.when((x == 0) & (y == 0) & (z == dz0) & (k == dk))
        def _():
            own = pltpu.make_async_copy(a.at[pl.ds(0, NB), pl.ds(0, NB)], dd.at[i], lsem.at[2])
            own.start()
            own.wait()

    pl.semaphore_wait(barrier, 7)

    def d_ways(i):
        dk, dz0 = roots[i]
        dz = (z + 8 - dz0) % 8
        line = (x == 0) & (y == 0)
        return (
            (ZP, line & (dz <= 3)),
            (ZM, line & ((dz == 0) | (dz >= 6))),
            (YP, (x == 0) & (y <= 1)),
            (YM, (x == 0) & (y == 0)),
            (XP, x <= 1),
            (XM, x == 0),
            (PA, x >= 0),
        )

    def d_copy(i, t, way):
        part = dd.at[i, pl.ds(pl.multiple_of(t * CH, CH), CH), :]
        return remote(part, part, dsend.at[way, i, t], drecv.at[i, t], way)

    def d_all():
        for i, (dk, dz0) in enumerate(roots):
            def step(t, carry):
                root = (x == 0) & (y == 0) & (z == dz0) & (k == dk)

                @pl.when(jnp.logical_not(root))
                def _():
                    d_copy(i, t, PA).wait_recv()

                for way, goes in d_ways(i):
                    @pl.when(goes & (k == dk))
                    def _():
                        d_copy(i, t, way).start()
                return carry
            lax.fori_loop(0, D_N, step, 0)

    def d_end():
        for i, (dk, dz0) in enumerate(roots):
            def step(t, carry):
                for way, goes in d_ways(i):
                    @pl.when(goes & (k == dk))
                    def _():
                        d_copy(i, t, way).wait_send()
                return carry
            lax.fori_loop(0, D_N, step, 0)

    p_ways = ((XP, x <= 1), (XM, x == 0), (PA, x >= 0))

    def p_copy(kk, t, way):
        part = pc.at[kk, pl.ds(pl.multiple_of(t * CH, CH), CH), :]
        return remote(part, part, psend.at[way - XP, t], precv.at[kk, t], way)

    def p_step(t):
        @pl.when(x > 0)
        def _():
            p_copy(k, t, XP).wait_recv()
        for way, goes in p_ways:
            @pl.when(goes)
            def _():
                p_copy(k, t, way).start()

    @pl.when(x == 0)
    def _():
        def step(t, carry):
            p_step(t)
            return carry
        lax.fori_loop(0, PC_N, step, 0)
        d_all()

    dz = (z + 8 - row) % 8
    source = dz == 0
    z_ways = ((ZP, dz <= 3), (ZM, source | (dz >= 6)))

    def r_part(ny, t):
        kk = (k + t // PC_N) % 2
        return rr.at[ny % 4, kk, pl.ds(pl.multiple_of((t % PC_N) * CH, CH), CH), :]

    def z_copy(t, way):
        return remote(r_part(y, t), r_part(y, t), zsend.at[way, t], zrecv.at[t], way)

    def y_copy(ny, t, way):
        slot = 0 if ny is y else 1
        return remote(
            r_part(ny, t), r_part(ny, t), ysend.at[way - YP, slot, t], yrecv.at[way - YP, slot, t],
            way,
        )

    def r_step(t):
        @pl.when(source)
        def _():
            @pl.when(t >= PC_N)
            def _():
                p_copy(1 - k, t - PC_N, PA).wait_recv()
            kk = (k + t // PC_N) % 2
            own = pltpu.make_async_copy(
                pc.at[kk, pl.ds(pl.multiple_of((t % PC_N) * CH, CH), CH), :],
                r_part(y, t), lsem.at[3],
            )
            own.start()
            own.wait()

        @pl.when(jnp.logical_not(source))
        def _():
            z_copy(t, ZP).wait_recv()
        for way, goes in z_ways:
            @pl.when(goes)
            def _():
                z_copy(t, way).start()
        y_copy(y, t, YP).start()
        y_copy(y, t, YM).start()

    def ring_step(t):
        below, above = y + 3, y + 1
        remote(r_part(below, t), r_part(below, t), ysend.at[0, 0, t], yrecv.at[0, 0, t], YP).wait_recv()
        remote(r_part(above, t), r_part(above, t), ysend.at[1, 0, t], yrecv.at[1, 0, t], YM).wait_recv()

        @pl.when(t % 2 == 0)
        def _():
            y_copy(below, t, YP).start()

        @pl.when(t % 2 == 1)
        def _():
            y_copy(above, t, YM).start()

    def main(t, carry):
        @pl.when((x > 0) & (t < PC_N))
        def _():
            p_step(t)

        @pl.when(t < R_N)
        def _():
            r_step(t)

        @pl.when(t >= LAG)
        def _():
            ring_step(t - LAG)
        return carry
    lax.fori_loop(0, R_N + LAG, main, 0)

    @pl.when(x > 0)
    def _():
        d_all()

    def finish(t, carry):
        across = y + 2

        @pl.when(t % 2 == 0)
        def _():
            y_copy(across, t, YP).wait_recv()
            y_copy(across, t, YP).wait_send()

        @pl.when(t % 2 == 1)
        def _():
            y_copy(across, t, YM).wait_recv()
            y_copy(across, t, YM).wait_send()
        y_copy(y, t, YP).wait_send()
        y_copy(y, t, YM).wait_send()
        for way, goes in z_ways:
            @pl.when(goes)
            def _():
                z_copy(t, way).wait_send()

        @pl.when(t < PC_N)
        def _():
            @pl.when(jnp.logical_not(source))
            def _():
                p_copy(1 - k, t, PA).wait_recv()
            for way, goes in p_ways:
                @pl.when(goes)
                def _():
                    p_copy(k, t, way).wait_send()
        return carry
    lax.fori_loop(0, R_N, finish, 0)
    d_end()


def gather(kernel):
    vmem = pl.BlockSpec(memory_space=pltpu.VMEM)
    dma = pltpu.SemaphoreType.DMA
    return pl.pallas_call(
        comm_kernel,
        out_shape=(
            jax.ShapeDtypeStruct((2, 512, NB), F32),
            jax.ShapeDtypeStruct((4, 2, 512, NB), F32),
            jax.ShapeDtypeStruct((3, NB, NB), F32),
        ),
        in_specs=[pl.BlockSpec(memory_space=pl.ANY)],
        out_specs=(vmem, vmem, vmem),
        scratch_shapes=[
            pltpu.VMEM((NB, 512), F32),
            pltpu.VMEM((512, NB), F32),
            dma((7, 3, D_N)),
            dma((3, D_N)),
            dma((3, PC_N)),
            dma((2, PC_N)),
            dma((2, R_N)),
            dma((R_N,)),
            dma((2, 2, R_N)),
            dma((2, 2, R_N)),
            dma((4,)),
        ],
        compiler_params=pltpu.CompilerParams(
            collective_id=0, has_side_effects=True, vmem_limit_bytes=32 << 20
        ),
        name="gather_panels",
    )(kernel)


def factor_slabs(fac):
    rows = lax.broadcasted_iota(jnp.int32, (8, 128), 0)
    for i in range(16):
        lo = 8 * i
        left = fac[lo : lo + 8, 0:128]
        right = fac[lo : lo + 8, 128:256]
        cols = [jnp.broadcast_to(left[:, lo + q : lo + q + 1], (8, 128)) for q in range(8)]
        for q in range(8):
            pivot = jnp.broadcast_to(cols[q][q : q + 1, :], (8, 128))
            inv = lax.rsqrt(pivot)
            coef = jnp.where(rows > q, cols[q] * inv, 0.0)
            scale = jnp.where(rows == q, inv, 1.0)
            u_left = jnp.broadcast_to(left[q : q + 1, :], (8, 128)) * inv
            u_right = jnp.broadcast_to(right[q : q + 1, :], (8, 128)) * inv
            left = left * scale - coef * u_left
            right = right * scale - coef * u_right
            for m in range(q + 1, 8):
                head = jnp.broadcast_to(cols[m][q : q + 1, :], (8, 128)) * inv
                cols[m] = cols[m] - coef * head
        fac[lo : lo + 8, 128:256] = right
        if i < 15:
            low = lo + 8
            wide = jnp.concatenate([left, right], axis=1)
            fac[low:128, :] = fac[low:128, :] - dot(left, wide, 0, 0)[low:128, :]


def factor_kernel(dd, pc, gt, low, mat, fac):
    col = lax.axis_index("col")
    ident = (
        lax.broadcasted_iota(jnp.int32, (128, 128), 0)
        == lax.broadcasted_iota(jnp.int32, (128, 128), 1)
    ).astype(F32)
    mat[...] = jnp.zeros_like(mat)
    for b in range(4):
        half, off = b // 2, b % 2 * 128
        mat[b, :, half * 256 : half * 256 + 256] = dd[2 * half, off : off + 128, :]
        if half == 0:
            mat[b, :, 256:512] = dd[1, off : off + 128, :]
        mat[b, :, 512 + 128 * b : 640 + 128 * b] = ident

    def block(b, carry):
        fac[:, 0:128] = mat[b, :, pl.ds(pl.multiple_of(b * 128, 128), 128)]
        fac[:, 128:256] = ident
        factor_slabs(fac)
        panel = dot(fac[:, 128:256], mat[b])
        mat[b] = panel

        def trail(i, c2):
            lhs = mat[b, :, pl.ds(pl.multiple_of(i * 128, 128), 128)]
            mat[i] = mat[i] - dot(lhs, mat[b], 0, 0)
            return c2
        lax.fori_loop(b + 1, 4, trail, 0)
        return carry
    lax.fori_loop(0, 4, block, 0)

    wide = mat[...].reshape(512, 1024)
    upper = wide[:, 0:512]
    winv = wide[:, 512:1024]
    tri = lax.broadcasted_iota(jnp.int32, (NB, NB), 0) >= lax.broadcasted_iota(jnp.int32, (NB, NB), 1)
    low[0] = jnp.where(tri, upper[0:256, 0:256].T, 0.0)
    low[1] = jnp.where(tri, upper[256:512, 256:512].T, 0.0)
    solved = dot(winv[:, 0:256], pc[0], 1, 1) + dot(winv[:, 256:512], pc[1], 1, 1)
    gt[...] = dot(winv, solved, 0, 0)

    @pl.when(col == 0)
    def _():
        gt[:, 0:256] = -winv[0:256, :].T

    @pl.when(col == 1)
    def _():
        gt[:, 0:256] = -winv[256:512, :].T


def factor(dd, pc):
    return pl.pallas_call(
        factor_kernel,
        out_shape=(
            jax.ShapeDtypeStruct((512, 512), F32),
            jax.ShapeDtypeStruct((2, NB, NB), F32),
        ),
        scratch_shapes=[pltpu.VMEM((4, 128, 1024), F32), pltpu.VMEM((128, 256), F32)],
        compiler_params=pltpu.CompilerParams(vmem_limit_bytes=48 << 20),
        name="factor_diagonal",
    )(dd, pc)


def update_kernel(a, rr, gt, low, out):
    row = lax.axis_index("row")
    col = lax.axis_index("col")
    slot = pl.program_id(0)
    acc = dot(rr[0, 0], gt[0:256, :]) + dot(rr[0, 1], gt[256:512, :])
    panel = (lax.broadcasted_iota(jnp.int32, (NB, 512), 1) < NB) & (col < 2)
    out[...] = jnp.where(panel, 0.0, a[...]) - acc

    @pl.when((slot == 0) & (row < 2))
    def _():
        out[:, 256:512] = jnp.zeros((NB, NB), F32)

        @pl.when(row == col)
        def _():
            out[:, 0:256] = low[row]

        @pl.when((col > 1) | ((row == 0) & (col == 1)))
        def _():
            out[:, 0:256] = jnp.zeros((NB, NB), F32)


def update(kernel, rr, gt, low):
    return pl.pallas_call(
        update_kernel,
        out_shape=jax.ShapeDtypeStruct(kernel.shape, F32),
        grid=(8,),
        in_specs=[
            pl.BlockSpec((NB, 512), lambda j: (j, 0)),
            pl.BlockSpec((1, 2, NB, NB), lambda j: (j % 4, 0, j // 4, 0)),
            pl.BlockSpec((512, 512), lambda j: (0, 0)),
            pl.BlockSpec((2, NB, NB), lambda j: (0, 0, 0)),
        ],
        out_specs=pl.BlockSpec((NB, 512), lambda j: (j, 0)),
        compiler_params=pltpu.CompilerParams(vmem_limit_bytes=48 << 20),
        name="update_trailing",
    )(kernel, rr, gt, low)


def local(kernel):
    pc, rr, dd = gather(kernel)
    gt, low = factor(dd, pc)
    return update(kernel, rr, gt, low)


def solution(mesh):
    placed = (P("row", "col"),)
    return jax.shard_map(
        local, mesh=mesh, in_specs=placed, out_specs=P("row", "col"), check_vma=False
    )
```

time: 782 us -> 136 us (0.17)
  the two profiles are of different devices: /device:TPU:103 before, /device:TPU:160 now
where the time goes in v1:
time: 136 us
  Pallas kernels  131 us (96%)
  local copies, waits for them, and re-layouts  4.12 us (3%)
    pallas_call x1, Pallas kernels, gather(): pl.pallas_call(comm_kernel, out_shape=(jax.ShapeDtypeStruct((2, 512, NB),...  76.8 us
    pallas_call x1, Pallas kernels, factor(): pl.pallas_call(factor_kernel, out_shape=(jax.ShapeDtypeStruct((512, 512),...  43.6 us
    pallas_call x1, Pallas kernels, update(): pl.pallas_call(update_kernel, out_shape=jax.ShapeDtypeStruct(kernel.shape...  11 us
    unnamed x6, local copies, waits for them, and re-layouts  4.12 us

profile of v1, /device:TPU:160, one launch (start us, length us, event | category | flops | bytes accessed | tf_op | source)
XLA Modules:
  0.0 135.5 jit_solution(2811995161733205321)
XLA Ops:
  0.0 0.0 copy-start
  0.0 2.2 %copy-done = f32[2048,512]{1,0:T(8,128)S(1)} copy-done((f32[2048,512]{1,0:T(8,128)S(1)}, f32[2048,512]{1,0:T(8,128)}, u32[]{:S(2)}) %copy-start) | copy-done | bytes 4194328
  2.2 0.0 copy-start.1
  2.2 76.8 %gather_panels.1 = (f32[2,512,256]{2,1,0:T(8,128)S(1)}, f32[4,2,512,256]{3,2,1,0:T(8,128)S(1)}, f32[3,256,256]{2,1,0:T(8,128)S(1)}) custom-call(f32[2048,512]{1,0:T(8,128)S(1)} %copy-done), custom_call_target="tpu_custom_call" | custom-call | tf_op jit(solution)/shard_map/gather_panels/pallas_call | solution.py:255
  79.0 0.0 copy-start.2
  79.0 1.9 %copy-done.2 = f32[4,2,512,256]{3,2,1,0:T(8,128)} copy-done((f32[4,2,512,256]{3,2,1,0:T(8,128)}, f32[4,2,512,256]{3,2,1,0:T(8,128)S(1)}, u32[]{:S(2)}) %copy-start.2) | copy-done | bytes 4194328
  80.9 43.6 %factor_diagonal.1 = (f32[512,512]{1,0:T(8,128)S(1)}, f32[2,256,256]{2,1,0:T(8,128)S(1)}) custom-call(f32[3,256,256]{2,1,0:T(8,128)S(1)} %get-tuple-element.11.dd, f32[2,512,256]{2,1,0:T(8,128)S(1)} %get-tuple-element.12.pc), custom_call_target="tpu_custom_call" | custom-call | tf_op jit(solution)/shard_map/factor_diagonal/pallas_call | solution.py:358
  124.5 0.0 copy-done.1
  124.5 11.0 %update_trailing.1 = f32[2048,512]{1,0:T(8,128)} custom-call(f32[2048,512]{1,0:T(8,128)S(1)} %copy-done.1, f32[4,2,512,256]{3,2,1,0:T(8,128)} %copy-done.2, f32[512,512]{1,0:T(8,128)S(1)} %get-tuple-element.13.gt, f32[2,256,256]{2,1,0:T(8,128)S(1)} %get-tuple-element.14.low), custom_call_target="tpu_custom_call" | custom-call | tf_op jit(solution)/shard_map/update_trailing/pallas_call | solution.py:392
Async XLA Ops:
  0.0 2.2 %copy-start = (f32[2048,512]{1,0:T(8,128)S(1)}, f32[2048,512]{1,0:T(8,128)}, u32[]{:S(2)}) copy-start(f32[2048,512]{1,0:T(8,128)} %a.3) | copy-start | bytes 12582916
  2.2 122.3 %copy-start.1 = (f32[2048,512]{1,0:T(8,128)S(1)}, f32[2048,512]{1,0:T(8,128)}, u32[]{:S(2)}) copy-start(f32[2048,512]{1,0:T(8,128)} %a.3) | copy-start | bytes 12582916
  79.0 1.9 %copy-start.2 = (f32[4,2,512,256]{3,2,1,0:T(8,128)}, f32[4,2,512,256]{3,2,1,0:T(8,128)S(1)}, u32[]{:S(2)}) copy-start(f32[4,2,512,256]{3,2,1,0:T(8,128)S(1)} %get-tuple-element.10.rr) | copy-start | bytes 12582916

commit v2 on v1

v2 whole, which is shorter than its diff:
```python
import jax
import jax.numpy as jnp
from jax import lax
from jax.experimental import pallas as pl
from jax.experimental.pallas import tpu as pltpu
from jax.sharding import PartitionSpec as P

NB = 256
F32 = jnp.float32
MESH = pl.DeviceIdType.MESH
HI = lax.Precision.HIGHEST

CH = 64
DH = 32
PC_N = 512 // CH
R_N = 2 * PC_N
D_N = NB // DH
LAG = 2
ZP, ZM, YP, YM, XP, XM, PA = range(7)


def dot(a, b, ca=1, cb=0):
    return lax.dot_general(
        a, b, (((ca,), (cb,)), ((), ())), precision=HI, preferred_element_type=F32
    )


def main_kernel(
    a, rr, gl, pc, oth, dd, head, headt, mat, fac,
    dsend, drecv, psend, precv, zsend, zrecv, ysend, yrecv, osend, orecv, gsend, grecv, lsem,
):
    row = lax.axis_index("row")
    col = lax.axis_index("col")
    x, k = row // 2, row % 2
    y, z = col // 8, col % 8

    def at(nx, ny, nz, nk):
        return ((nx % 4) * 2 + nk, (ny % 4) * 8 + nz % 8)

    near = {
        ZP: at(x, y, z + 1, 1),
        ZM: at(x, y, z + 7, 1),
        YP: at(x, y + 1, z, 1),
        YM: at(x, y + 3, z, 1),
        XP: at(x + 1, y, z, 1),
        XM: at(x + 3, y, z, 1),
        PA: at(x, y, z, 1 - k),
    }
    barrier = pltpu.get_barrier_semaphore()

    def greet(target):
        pl.semaphore_signal(barrier, inc=1, device_id=target, device_id_type=MESH)

    for way in (XP, XM, PA):
        greet(near[way])

    @pl.when(k == 1)
    def _():
        for way in (ZP, ZM, YP, YM):
            greet(near[way])
        greet(at(x + 1, y, z, 0))
        greet(at(x + 3, y, z, 0))

    def remote(src, dst, send, recv, way):
        return pltpu.make_async_remote_copy(
            src_ref=src, dst_ref=dst, send_sem=send, recv_sem=recv,
            device_id=near[way], device_id_type=MESH,
        )

    def rows_of(t, size):
        return pl.ds(pl.multiple_of(t * size, size), size)

    @pl.when(x == 0)
    def _():
        load = pltpu.make_async_copy(a.at[pl.ds(0, NB), :], head, lsem.at[0])
        load.start()
        load.wait()
        headt[...] = head[...].T

    @pl.when((x == 0) & (y == 0) & (z < 2) & ((k == 0) | (z == 1)))
    def _():
        own = pltpu.make_async_copy(
            a.at[pl.ds(0, NB), pl.ds(0, NB)], dd.at[z + k], lsem.at[1]
        )
        own.start()
        own.wait()

    def d_root(i):
        return (x == 0) & (y == 0) & (z == jnp.minimum(i, 1))

    def d_ways(i):
        dz = (z + 8 - jnp.minimum(i, 1)) % 8
        line = (x == 0) & (y == 0)
        return (
            (ZP, line & (dz <= 3)),
            (ZM, line & ((dz == 0) | (dz >= 6))),
            (YP, (x == 0) & (y <= 1)),
            (YM, (x == 0) & (y == 0)),
            (XP, x <= 1),
            (XM, x == 0),
            (PA, jnp.logical_not(d_root(i) & (i < 2))),
        )

    def d_copy(i, t, way):
        part = dd.at[i, rows_of(t, DH), :]
        return remote(part, part, dsend.at[way, i, t], drecv.at[i, t], way)

    def d_step(u):
        i, t = u // D_N, u % D_N

        @pl.when(jnp.logical_not(d_root(i) & (i == 2)))
        def _():
            d_copy(i, t, PA).wait_recv()

        for way, goes in d_ways(i):
            @pl.when(goes)
            def _():
                d_copy(i, t, way).start()

    def p_copy(kk, t, way):
        part = pc.at[kk, rows_of(t, CH), :]
        return remote(part, part, psend.at[way - XP, kk, t], precv.at[kk, t], way)

    def p_first(t, way):
        return remote(
            headt.at[rows_of(t, CH), :], pc.at[k, rows_of(t, CH), :],
            psend.at[way - XP, k, t], precv.at[k, t], way,
        )

    def fill_own():
        return pltpu.make_async_copy(headt, pc.at[k], lsem.at[2])

    def p_step(kk, t):
        p_copy(kk, t, XP).wait_recv()

        @pl.when(x == 1)
        def _():
            p_copy(kk, t, XP).start()
        p_copy(kk, t, PA).start()

    def held(g):
        return rr if g else oth

    def source(g):
        return z == 2 * x + g

    def z_ways(g):
        dz = (z + 8 - 2 * x - g) % 8
        return ((ZP, dz <= 3), (ZM, (dz == 0) | (dz >= 6)))

    def r_part(buf, ny, t):
        return buf.at[ny % 4, t % 2, rows_of(t // 2, CH), :]

    def z_copy(g, t, way):
        part = r_part(held(g), y, t)
        return remote(part, part, zsend.at[way, g, t], zrecv.at[g, t], way)

    def y_copy(g, ny, t, way, slot):
        part = r_part(held(g), ny, t)
        return remote(
            part, part, ysend.at[way - YP, slot, g, t], yrecv.at[way - YP, slot, g, t], way
        )

    def o_copy(ny, t):
        ny = ny % 4
        return remote(
            r_part(oth, ny, t), r_part(rr, ny, t), osend.at[ny, t], orecv.at[ny, t], PA
        )

    def r_step(g, t):
        @pl.when(source(g))
        def _():
            own = pltpu.make_async_copy(
                pc.at[t % 2, rows_of(t // 2, CH), :], r_part(held(g), y, t), lsem.at[3]
            )
            own.start()
            own.wait()

        @pl.when(jnp.logical_not(source(g)))
        def _():
            z_copy(g, t, ZP).wait_recv()
        for way, goes in z_ways(g):
            @pl.when(goes)
            def _():
                z_copy(g, t, way).start()
        y_copy(g, y, t, YP, 0).start()
        y_copy(g, y, t, YM, 0).start()
        if g == 0:
            o_copy(y, t).start()

    def ring_step(g, t):
        y_copy(g, y + 3, t, YP, 0).wait_recv()
        y_copy(g, y + 1, t, YM, 0).wait_recv()

        @pl.when(t // 2 % 2 == 0)
        def _():
            y_copy(g, y + 3, t, YP, 1).start()

        @pl.when(t // 2 % 2 == 1)
        def _():
            y_copy(g, y + 1, t, YM, 1).start()
        if g == 0:
            o_copy(y + 3, t).start()
            o_copy(y + 1, t).start()

    def last_step(g, t):
        @pl.when(t // 2 % 2 == 0)
        def _():
            y_copy(g, y + 2, t, YP, 1).wait_recv()

        @pl.when(t // 2 % 2 == 1)
        def _():
            y_copy(g, y + 2, t, YM, 1).wait_recv()
        if g == 0:
            o_copy(y + 2, t).start()

    def loop(n, body):
        def step(t, carry):
            body(t)
            return carry
        lax.fori_loop(0, n, step, 0)

    def g_copy(h):
        part = gl.at[pl.ds(256 * h, 256), :]
        return remote(part, part, gsend.at[h], grecv.at[h], PA)

    @pl.when(k == 1)
    def _carry():
        pl.semaphore_wait(barrier, 9)

        @pl.when(x == 0)
        def _():
            fill_own().start()

            def first(t):
                for way in (XP, XM, PA):
                    p_first(t, way).start()
            loop(PC_N, first)
            fill_own().wait()
            loop(3 * D_N, d_step)

        begin = jnp.where(x == 2, 4, 1)

        def body(t):
            @pl.when(t < R_N)
            def _():
                @pl.when(x > 0)
                def _():
                    p_step(t % 2, t // 2)

                @pl.when((x == 0) & (t % 2 == 0))
                def _():
                    p_copy(0, t // 2, PA).wait_recv()
                r_step(0, t)
                r_step(1, t)

            @pl.when((x > 0) & (t >= begin) & (t < begin + 6))
            def _():
                def four(q):
                    d_step(4 * (t - begin) + q)
                loop(4, four)

            @pl.when(t >= LAG)
            def _():
                ring_step(0, t - LAG)
                ring_step(1, t - LAG)

            @pl.when(t >= 2 * LAG)
            def _():
                last_step(0, t - 2 * LAG)
                last_step(1, t - 2 * LAG)
        def guarded(t):
            @pl.when(t < R_N + LAG)
            def _():
                body(t)

            @pl.when(t >= R_N + LAG)
            def _():
                last_step(0, t - 2 * LAG)
                last_step(1, t - 2 * LAG)
        loop(R_N + 2 * LAG, guarded)

        def finish(t):
            for g in range(2):
                for way, goes in z_ways(g):
                    @pl.when(goes)
                    def _():
                        z_copy(g, t, way).wait_send()
                y_copy(g, y, t, YP, 0).wait_send()
                y_copy(g, y, t, YM, 0).wait_send()

                @pl.when(t // 2 % 2 == 0)
                def _():
                    y_copy(g, y + 3, t, YP, 1).wait_send()

                @pl.when(t // 2 % 2 == 1)
                def _():
                    y_copy(g, y + 1, t, YM, 1).wait_send()
            for q in range(4):
                o_copy(y + q, t).wait_send()

            @pl.when(x == 0)
            def _():
                @pl.when(t < PC_N)
                def _():
                    for way in (XP, XM, PA):
                        p_first(t, way).wait_send()

            @pl.when(x == 1)
            def _():
                p_copy(t % 2, t // 2, XP).wait_send()

            @pl.when(x > 0)
            def _():
                p_copy(t % 2, t // 2, PA).wait_send()
        loop(R_N, finish)

        def d_end(u):
            i, t = u // D_N, u % D_N
            for way, goes in d_ways(i):
                @pl.when(goes)
                def _():
                    d_copy(i, t, way).wait_send()
        loop(3 * D_N, d_end)
        for h in range(3):
            g_copy(h).wait_recv()

    @pl.when(k == 0)
    def _factor():
        pl.semaphore_wait(barrier, 3)
        mine = (x == 0) & (y == 0) & (z < 2)

        @pl.when(mine)
        def _():
            def send(t):
                d_copy(z, t, PA).start()
            loop(D_N, send)

        @pl.when(x == 0)
        def _():
            def first(t):
                for way in (PA, XP, XM):
                    p_first(t, way).start()
            loop(PC_N, first)
            fill_own().start()

        def d_wait(i):
            @pl.when(jnp.logical_not(d_root(i) & (i < 2)))
            def _():
                def one(t):
                    d_copy(i, t, PA).wait_recv()
                loop(D_N, one)

        def panel_wait():
            @pl.when(x == 0)
            def _():
                fill_own().wait()

            @pl.when(x > 0)
            def _():
                def one(t):
                    p_copy(0, t, PA).wait_recv()
                loop(PC_N, one)

            def other(t):
                p_copy(1, t, PA).wait_recv()
            loop(PC_N, other)

        factor(dd, pc, gl, mat, fac, col, d_wait, panel_wait, lambda h: g_copy(h).start())

        def rest(t):
            for q in range(4):
                o_copy(q, t).wait_recv()
        loop(R_N, rest)

        @pl.when(mine)
        def _():
            def sent(t):
                d_copy(z, t, PA).wait_send()
            loop(D_N, sent)

        @pl.when(x == 0)
        def _():
            def sent(t):
                for way in (PA, XP, XM):
                    p_first(t, way).wait_send()
            loop(PC_N, sent)
        for h in range(3):
            g_copy(h).wait_send()


def gather_and_factor(kernel):
    vmem = pl.BlockSpec(memory_space=pltpu.VMEM)
    dma = pltpu.SemaphoreType.DMA
    return pl.pallas_call(
        main_kernel,
        out_shape=(
            jax.ShapeDtypeStruct((4, 2, 512, NB), F32),
            jax.ShapeDtypeStruct((768, 512), F32),
        ),
        in_specs=[pl.BlockSpec(memory_space=pltpu.HBM)],
        out_specs=(vmem, vmem),
        scratch_shapes=[
            pltpu.VMEM((2, 512, NB), F32),
            pltpu.VMEM((4, 2, 512, NB), F32),
            pltpu.VMEM((3, NB, NB), F32),
            pltpu.VMEM((NB, 512), F32),
            pltpu.VMEM((512, NB), F32),
            pltpu.VMEM((4, 128, 1024), F32),
            pltpu.VMEM((128, 256), F32),
            dma((7, 3, D_N)),
            dma((3, D_N)),
            dma((3, 2, PC_N)),
            dma((2, PC_N)),
            dma((2, 2, R_N)),
            dma((2, R_N)),
            dma((2, 2, 2, R_N)),
            dma((2, 2, 2, R_N)),
            dma((4, R_N)),
            dma((4, R_N)),
            dma((3,)),
            dma((3,)),
            dma((4,)),
        ],
        compiler_params=pltpu.CompilerParams(
            collective_id=0, has_side_effects=True, vmem_limit_bytes=56 << 20
        ),
        name="gather_and_factor",
    )(kernel)


def factor_slabs(fac):
    rows = lax.broadcasted_iota(jnp.int32, (8, 128), 0)
    for i in range(16):
        lo = 8 * i
        left = fac[lo : lo + 8, 0:128]
        right = fac[lo : lo + 8, 128:256]
        cols = [jnp.broadcast_to(left[:, lo + q : lo + q + 1], (8, 128)) for q in range(8)]
        for q in range(8):
            pivot = jnp.broadcast_to(cols[q][q : q + 1, :], (8, 128))
            inv = lax.rsqrt(pivot)
            coef = jnp.where(rows > q, cols[q] * inv, 0.0)
            scale = jnp.where(rows == q, inv, 1.0)
            u_left = jnp.broadcast_to(left[q : q + 1, :], (8, 128)) * inv
            u_right = jnp.broadcast_to(right[q : q + 1, :], (8, 128)) * inv
            left = left * scale - coef * u_left
            right = right * scale - coef * u_right
            for m in range(q + 1, 8):
                head = jnp.broadcast_to(cols[m][q : q + 1, :], (8, 128)) * inv
                cols[m] = cols[m] - coef * head
        fac[lo : lo + 8, 128:256] = right
        if i < 15:
            low = lo + 8
            wide = jnp.concatenate([left, right], axis=1)
            fac[low:128, :] = fac[low:128, :] - dot(left, wide, 0, 0)[low:128, :]


def factor(dd, pc, gl, mat, fac, col, d_wait, panel_wait, send):
    ident = (
        lax.broadcasted_iota(jnp.int32, (128, 128), 0)
        == lax.broadcasted_iota(jnp.int32, (128, 128), 1)
    ).astype(F32)
    mat[...] = jnp.zeros_like(mat)
    for b in range(4):
        mat[b, :, 512 + 128 * b : 640 + 128 * b] = ident
    d_wait(0)
    for b in range(2):
        mat[b, :, 0:256] = dd[0, 128 * b : 128 * b + 128, :]

    def block(b, carry):
        fac[:, 0:128] = mat[b, :, pl.ds(pl.multiple_of(b * 128, 128), 128)]
        fac[:, 128:256] = ident
        factor_slabs(fac)

        @pl.when(b == 0)
        def _():
            d_wait(1)
            d_wait(2)
            for q in range(2):
                mat[q, :, 256:512] = dd[1, 128 * q : 128 * q + 128, :]
                mat[q + 2, :, 256:512] = dd[2, 128 * q : 128 * q + 128, :]
        panel = dot(fac[:, 128:256], mat[b])
        mat[b] = panel

        def trail(i, c2):
            lhs = mat[b, :, pl.ds(pl.multiple_of(i * 128, 128), 128)]
            mat[i] = mat[i] - dot(lhs, mat[b], 0, 0)
            return c2
        lax.fori_loop(b + 1, 4, trail, 0)
        return carry
    lax.fori_loop(0, 4, block, 0)

    wide = mat[...].reshape(512, 1024)
    winv = wide[:, 512:1024]
    tri = lax.broadcasted_iota(jnp.int32, (NB, NB), 0) >= lax.broadcasted_iota(jnp.int32, (NB, NB), 1)
    for h in range(2):
        own = slice(256 * h, 256 * h + 256)
        gl[512:768, own] = jnp.where(tri, wide[own, own].T, 0.0)
    send(2)
    panel_wait()
    solved = dot(winv[:, 0:256], pc[0], 1, 1) + dot(winv[:, 256:512], pc[1], 1, 1)
    for h in range(2):
        rows = slice(256 * h, 256 * h + 256)
        gl[rows, :] = dot(winv[:, rows], solved, 0, 0)
        for q in range(2):
            @pl.when(col == q)
            def _():
                gl[rows, 0:256] = -winv[256 * q : 256 * q + 256, rows].T
        send(h)


def update_kernel(a, rr, gl, out, hi, lo):
    row = lax.axis_index("row")
    col = lax.axis_index("col")
    slot = pl.program_id(0)

    @pl.when(slot == 0)
    def _():
        g = gl[0:512, :]
        top = g.astype(jnp.bfloat16)
        hi[...] = top
        lo[...] = (g - top.astype(F32)).astype(jnp.bfloat16)

    def mul(p, q):
        return jnp.dot(p, q, preferred_element_type=F32)

    acc = jnp.zeros((NB, 512), F32)
    for kk in range(2):
        r = rr[slot % 4, kk, pl.ds(pl.multiple_of(slot // 4 * NB, NB), NB), :]
        top = r.astype(jnp.bfloat16)
        rest = (r - top.astype(F32)).astype(jnp.bfloat16)
        rows = slice(kk * NB, kk * NB + NB)
        acc = acc + mul(top, hi[rows, :]) + (mul(top, lo[rows, :]) + mul(rest, hi[rows, :]))
    panel = (lax.broadcasted_iota(jnp.int32, (NB, 512), 1) < NB) & (col < 2)
    out[...] = jnp.where(panel, 0.0, a[...]) - acc

    @pl.when((slot == 0) & (row < 2))
    def _():
        out[:, 256:512] = jnp.zeros((NB, NB), F32)
        for q in range(2):
            @pl.when((row == q) & (col == q))
            def _():
                out[:, 0:256] = gl[512:768, 256 * q : 256 * q + 256]

        @pl.when((col > 1) | ((row == 0) & (col == 1)))
        def _():
            out[:, 0:256] = jnp.zeros((NB, NB), F32)


def update(kernel, rr, gl):
    vmem = pl.BlockSpec(memory_space=pltpu.VMEM)
    return pl.pallas_call(
        update_kernel,
        out_shape=jax.ShapeDtypeStruct(kernel.shape, F32),
        grid=(8,),
        in_specs=[pl.BlockSpec((NB, 512), lambda j: (j, 0)), vmem, vmem],
        out_specs=pl.BlockSpec((NB, 512), lambda j: (j, 0)),
        scratch_shapes=[pltpu.VMEM((512, 512), jnp.bfloat16)] * 2,
        compiler_params=pltpu.CompilerParams(vmem_limit_bytes=24 << 20),
        name="update_trailing",
    )(kernel, rr, gl)


def local(kernel):
    rr, gl = gather_and_factor(kernel)
    return update(kernel, rr, gl)


def solution(mesh):
    placed = (P("row", "col"),)
    return jax.shard_map(
        local, mesh=mesh, in_specs=placed, out_specs=P("row", "col"), check_vma=False
    )
```

time: 136 us -> 132 us (0.971)
  the two profiles are of different devices: /device:TPU:160 before, /device:TPU:161 now
where the time goes in v2:
time: 132 us
  Pallas kernels  128 us (97%)
  local copies, waits for them, and re-layouts  3.59 us (3%)
    pallas_call x1, Pallas kernels, gather_and_factor(): pl.pallas_call(main_kernel, out_shape=(jax.ShapeDtypeStruct((4, 2, 512, N...  122 us
    pallas_call x1, Pallas kernels, update(): pl.pallas_call(update_kernel, out_shape=jax.ShapeDtypeStruct(kernel.shape...  6.23 us
    unnamed x6, local copies, waits for them, and re-layouts  3.59 us

profile of v2, /device:TPU:161, one launch (start us, length us, event | category | flops | bytes accessed | tf_op | source)
XLA Modules:
  0.0 131.6 jit_solution(10439998729225748086)
XLA Ops:
  0.0 0.0 copy-start
  0.0 121.7 %gather_and_factor.1 = (f32[4,2,512,256]{3,2,1,0:T(8,128)}, f32[768,512]{1,0:T(8,128)}) custom-call(f32[2048,512]{1,0:T(8,128)} %a.3), custom_call_target="tpu_custom_call" | custom-call | tf_op jit(solution)/shard_map/gather_and_factor/pallas_call | solution.py:395
  121.8 0.0 copy-done
  121.8 0.0 copy-start.1
  121.8 2.2 %copy-done.1 = f32[4,2,512,256]{3,2,1,0:T(8,128)S(1)} copy-done((f32[4,2,512,256]{3,2,1,0:T(8,128)S(1)}, f32[4,2,512,256]{3,2,1,0:T(8,128)}, u32[]{:S(2)}) %copy-start.1) | copy-done | bytes 4194328
  124.0 0.0 copy-start.2
  124.0 1.4 %copy-done.2 = f32[768,512]{1,0:T(8,128)S(1)} copy-done((f32[768,512]{1,0:T(8,128)S(1)}, f32[768,512]{1,0:T(8,128)}, u32[]{:S(2)}) %copy-start.2) | copy-done | bytes 1572888
  125.4 6.2 %update_trailing.1 = f32[2048,512]{1,0:T(8,128)} custom-call(f32[2048,512]{1,0:T(8,128)S(1)} %copy-done, f32[4,2,512,256]{3,2,1,0:T(8,128)S(1)} %copy-done.1, f32[768,512]{1,0:T(8,128)S(1)} %copy-done.2), custom_call_target="tpu_custom_call" | custom-call | tf_op jit(solution)/shard_map/update_trailing/pallas_call | solution.py:552
Async XLA Ops:
  0.0 121.8 %copy-start = (f32[2048,512]{1,0:T(8,128)S(1)}, f32[2048,512]{1,0:T(8,128)}, u32[]{:S(2)}) copy-start(f32[2048,512]{1,0:T(8,128)} %a.3) | copy-start | bytes 12582916
  121.8 2.2 %copy-start.1 = (f32[4,2,512,256]{3,2,1,0:T(8,128)S(1)}, f32[4,2,512,256]{3,2,1,0:T(8,128)}, u32[]{:S(2)}) copy-start(f32[4,2,512,256]{3,2,1,0:T(8,128)} %get-tuple-element.7.rr) | copy-start | bytes 12582916
  124.0 1.4 %copy-start.2 = (f32[768,512]{1,0:T(8,128)S(1)}, f32[768,512]{1,0:T(8,128)}, u32[]{:S(2)}) copy-start(f32[768,512]{1,0:T(8,128)} %get-tuple-element.8.gl) | copy-start | bytes 4718596

commit v3 on v2

v3 whole, which is shorter than its diff:
```python
import jax
import jax.numpy as jnp
from jax import lax
from jax.experimental import pallas as pl
from jax.experimental.pallas import tpu as pltpu
from jax.sharding import PartitionSpec as P

NB = 256
F32 = jnp.float32
MESH = pl.DeviceIdType.MESH
HI = lax.Precision.HIGHEST

CH = 64
DH = 32
PC_N = 512 // CH
D_N = NB // DH
LAGS = (0, 1, 2, 3)
ZP, ZM, YP, YM, XP, XM, PA, CP, CM = range(9)


def dot(a, b, ca=1, cb=0):
    return lax.dot_general(
        a, b, (((ca,), (cb,)), ((), ())), precision=HI, preferred_element_type=F32
    )


def main_kernel(
    a, rr, gl, pc, oth, dd, head, headt, mat, fac,
    dsend, drecv, psend, precv, ppass, zsend, zrecv, ysend, yrecv,
    osend, orecv, gsend, grecv, lsem,
):
    row = lax.axis_index("row")
    col = lax.axis_index("col")
    x, k = row // 2, row % 2
    y, z = col // 8, col % 8

    def at(nx, ny, nz, nk):
        return ((nx % 4) * 2 + nk, (ny % 4) * 8 + nz % 8)

    near = {
        ZP: at(x, y, z + 1, k),
        ZM: at(x, y, z + 7, k),
        YP: at(x, y + 1, z, k),
        YM: at(x, y + 3, z, k),
        XP: at(x + 1, y, z, k),
        XM: at(x + 3, y, z, k),
        PA: at(x, y, z, 1 - k),
        CP: at(x + 1, y, z, 1),
        CM: at(x + 3, y, z, 1),
    }
    barrier = pltpu.get_barrier_semaphore()
    for target in [near[way] for way in range(7)] + [
        at(x + 1, y, z, 1 - k), at(x + 3, y, z, 1 - k)
    ]:
        pl.semaphore_signal(barrier, inc=1, device_id=target, device_id_type=MESH)

    def remote(src, dst, send, recv, way):
        return pltpu.make_async_remote_copy(
            src_ref=src, dst_ref=dst, send_sem=send, recv_sem=recv,
            device_id=near[way], device_id_type=MESH,
        )

    def rows_of(t, size):
        return pl.ds(pl.multiple_of(t * size, size), size)

    @pl.when(x == 0)
    def _():
        load = pltpu.make_async_copy(a.at[pl.ds(0, NB), :], head, lsem.at[0])
        load.start()
        load.wait()
        headt[...] = head[...].T

    @pl.when((x == 0) & (y == 0) & (z < 2) & ((k == 0) | (z == 1)))
    def _():
        own = pltpu.make_async_copy(
            a.at[pl.ds(0, NB), pl.ds(0, NB)], dd.at[z + k], lsem.at[1]
        )
        own.start()
        own.wait()

    below, above, across = (y + 3) % 4, (y + 1) % 4, (y + 2) % 4

    def loop(n, body, first=0):
        def step(t, carry):
            body(t)
            return carry
        lax.fori_loop(first, n, step, 0)

    d_root, d_ways = [], []
    for i in range(3):
        dz = (z + 8 - min(i, 1)) % 8
        line = (x == 0) & (y == 0)
        root = line & (dz == 0)
        d_root.append(root)
        d_ways.append((
            (ZP, line & (dz <= 3)),
            (ZM, line & ((dz == 0) | (dz >= 6))),
            (YP, (x == 0) & (y <= 1)),
            (YM, (x == 0) & (y == 0)),
            (XP, x <= 1),
            (XM, x == 0),
        ))

    def d_copy(i, t, way):
        part = dd.at[i, rows_of(t, DH), :]
        return remote(part, part, dsend.at[way, i], drecv.at[i, t], way)

    def d_whole(i, way):
        return remote(dd.at[i], dd.at[i], dsend.at[way, i], drecv.at[i, 0], way)

    def d_block(i):
        def one(t):
            if i == 2:
                d_copy(i, t, PA).wait_recv()
            else:
                @pl.when(jnp.logical_not(d_root[i]))
                def _():
                    d_copy(i, t, PA).wait_recv()

            for way, goes in d_ways[i]:
                @pl.when(goes)
                def _():
                    d_copy(i, t, way).start()
        loop(D_N, one)

    def p_copy(kk, t, way):
        part = pc.at[kk, rows_of(t, CH), :]
        return remote(part, part, psend.at[way - PA, kk], precv.at[kk, t], way)

    def p_pass(kk, t):
        part = pc.at[kk, rows_of(t, CH), :]
        return remote(part, part, psend.at[0, kk], ppass.at[kk], PA)

    def p_whole(kk, way):
        return remote(pc.at[kk], pc.at[kk], psend.at[way - PA, kk], ppass.at[kk], way)

    def p_first(kk, t, way):
        recv = ppass.at[kk] if (way == PA and kk == 1) else precv.at[kk, t]
        return remote(
            headt.at[rows_of(t, CH), :], pc.at[kk, rows_of(t, CH), :],
            psend.at[way - PA, kk], recv, way,
        )

    def fill_own(kk):
        return pltpu.make_async_copy(headt, pc.at[kk], lsem.at[2])

    def p_step(kk, t):
        p_copy(kk, t, PA).wait_recv()

        @pl.when(x == 1)
        def _():
            p_copy(kk, t, CP).start()
        p_pass(kk, t).start()

    held = (oth, rr)
    source = [z == 2 * x + g for g in range(2)]
    z_ways = []
    for g in range(2):
        dz = (z + 8 - 2 * x - g) % 8
        z_ways.append(((ZP, dz <= 3), (ZM, (dz == 0) | (dz >= 6))))

    def r_part(buf, ny, kk, t):
        return buf.at[ny, kk, rows_of(t, CH), :]

    def z_copy(g, kk, t, way):
        part = r_part(held[g], y, kk, t)
        return remote(part, part, zsend.at[way, g], zrecv.at[g, kk, t], way)

    def y_copy(g, ny, kk, t, way, slot):
        part = r_part(held[g], ny, kk, t)
        return remote(
            part, part, ysend.at[way - YP, slot, g], yrecv.at[way - YP, slot, g, kk, t], way
        )

    def o_copy(ny, kk, t):
        return remote(
            r_part(oth, ny, kk, t), r_part(rr, ny, kk, t), osend.at[0], orecv.at[0], PA
        )

    def own_step(g, kk, t):
        part = pc.at[kk, rows_of(t, CH), :]
        pltpu.make_async_copy(part, r_part(held[g], y, kk, t), lsem.at[3]).start()
        dst = r_part(held[g], y, kk, t)
        for way in (ZP, ZM):
            remote(part, dst, zsend.at[way, g], zrecv.at[g, kk, t], way).start()
        for way in (YP, YM):
            remote(
                part, dst, ysend.at[way - YP, 0, g], yrecv.at[way - YP, 0, g, kk, t], way
            ).start()
        if g == 0:
            remote(part, r_part(rr, y, kk, t), osend.at[0], orecv.at[0], PA).start()

    def pass_step(g, kk, t):
        z_copy(g, kk, t, ZP).wait_recv()
        for way, goes in z_ways[g]:
            @pl.when(goes)
            def _():
                z_copy(g, kk, t, way).start()
        y_copy(g, y, kk, t, YP, 0).start()
        y_copy(g, y, kk, t, YM, 0).start()
        if g == 0:
            o_copy(y, kk, t).start()

    def ring_step(g, kk, t):
        y_copy(g, below, kk, t, YP, 0).wait_recv()
        y_copy(g, above, kk, t, YM, 0).wait_recv()
        if kk == 0:
            y_copy(g, below, kk, t, YP, 1).start()
        else:
            y_copy(g, above, kk, t, YM, 1).start()
        if g == 0:
            o_copy(below, kk, t).start()
            o_copy(above, kk, t).start()

    def last_step(g, kk, t):
        y_copy(g, across, kk, t, YM if kk else YP, 1).wait_recv()
        if g == 0:
            o_copy(across, kk, t).start()

    def g_copy(h):
        part = gl.at[pl.ds(256 * h, 256), :]
        return remote(part, part, gsend.at[h], grecv.at[h], PA)

    @pl.when(k == 1)
    def _carry():
        pl.semaphore_wait(barrier, 9)

        @pl.when(d_root[2])
        def _():
            loop(D_N, lambda t: d_copy(2, t, PA).start())

        @pl.when(x == 0)
        def _():
            fill_own(1).start()

            def first(t):
                for way in (CP, CM, PA):
                    p_first(1, t, way).start()
            loop(PC_N, first)
            fill_own(1).wait()

        def stage0(t):
            for kk in range(2):
                @pl.when(x > 0)
                def _():
                    p_step(kk, t)
                if kk == 0:
                    @pl.when(x == 0)
                    def _():
                        p_copy(0, t, PA).wait_recv()
                for g in range(2):
                    @pl.when(source[g])
                    def _():
                        own_step(g, kk, t)

        def stage1(t):
            for kk in range(2):
                for g in range(2):
                    @pl.when(jnp.logical_not(source[g]))
                    def _():
                        pass_step(g, kk, t)

        def stage2(t):
            for kk in range(2):
                for g in range(2):
                    ring_step(g, kk, t)

        def stage3(t):
            for kk in range(2):
                for g in range(2):
                    last_step(g, kk, t)

        def body(t):
            for lag, stage in enumerate((stage0, stage1, stage2, stage3)):
                at_t = LAGS[lag]

                @pl.when((t >= at_t) & (t < PC_N + at_t))
                def _():
                    stage(t - at_t)
        loop(PC_N + LAGS[-1], body)

        for g in range(2):
            @pl.when(source[g])
            def _():
                pltpu.make_async_copy(pc, held[g].at[y], lsem.at[3]).wait()
        for g in range(2):
            for way, goes in z_ways[g]:
                @pl.when(goes)
                def _():
                    remote(rr.at[0], rr.at[0], zsend.at[way, g], orecv.at[0], way).wait_send()
            for way in (YP, YM):
                remote(rr.at[0], rr.at[0], ysend.at[way - YP, 0, g], orecv.at[0], way).wait_send()
                half = rr.at[0, 0]
                remote(half, half, ysend.at[way - YP, 1, g], orecv.at[0], way).wait_send()
        remote(oth, rr, osend.at[0], orecv.at[0], PA).wait_send()

        @pl.when(x == 0)
        def _():
            for way in (CP, CM, PA):
                p_whole(1, way).wait_send()

        @pl.when(x > 0)
        def _():
            for kk in range(2):
                @pl.when(x == 1)
                def _():
                    p_whole(kk, CP).wait_send()
                p_whole(kk, PA).wait_send()

        @pl.when(d_root[2])
        def _():
            d_whole(2, PA).wait_send()
        for h in range(3):
            g_copy(h).wait_recv()

    @pl.when(k == 0)
    def _factor():
        pl.semaphore_wait(barrier, 9)

        @pl.when(x == 0)
        def _():
            def first(t):
                for way in (PA, CP, CM):
                    p_first(0, t, way).start()
            loop(PC_N, first)
            fill_own(0).start()
        for i in range(3):
            d_block(i)

        def panel_wait():
            @pl.when(x == 0)
            def _():
                fill_own(0).wait()

            @pl.when(x > 0)
            def _():
                p_whole(0, PA).wait_recv()
            p_whole(1, PA).wait_recv()

        factor(dd, pc, gl, mat, fac, col, panel_wait, lambda h: g_copy(h).start())

        remote(oth, rr, osend.at[0], orecv.at[0], PA).wait_recv()
        for i in range(3):
            for way, goes in d_ways[i]:
                @pl.when(goes)
                def _():
                    d_whole(i, way).wait_send()

        @pl.when(x == 0)
        def _():
            for way in (PA, CP, CM):
                p_whole(0, way).wait_send()
        for h in range(3):
            g_copy(h).wait_send()


def gather_and_factor(kernel):
    vmem = pl.BlockSpec(memory_space=pltpu.VMEM)
    dma = pltpu.SemaphoreType.DMA
    return pl.pallas_call(
        main_kernel,
        out_shape=(
            jax.ShapeDtypeStruct((4, 2, 512, NB), F32),
            jax.ShapeDtypeStruct((768, 512), F32),
        ),
        in_specs=[pl.BlockSpec(memory_space=pltpu.HBM)],
        out_specs=(vmem, vmem),
        scratch_shapes=[
            pltpu.VMEM((2, 512, NB), F32),
            pltpu.VMEM((4, 2, 512, NB), F32),
            pltpu.VMEM((3, NB, NB), F32),
            pltpu.VMEM((NB, 512), F32),
            pltpu.VMEM((512, NB), F32),
            pltpu.VMEM((4, 128, 1024), F32),
            pltpu.VMEM((128, 256), F32),
            dma((7, 3)),
            dma((3, D_N)),
            dma((3, 2)),
            dma((2, PC_N)),
            dma((2,)),
            dma((2, 2)),
            dma((2, 2, PC_N)),
            dma((2, 2, 2)),
            dma((2, 2, 2, 2, PC_N)),
            dma((1,)),
            dma((1,)),
            dma((3,)),
            dma((3,)),
            dma((4,)),
        ],
        compiler_params=pltpu.CompilerParams(
            collective_id=0, has_side_effects=True, vmem_limit_bytes=56 << 20
        ),
        name="gather_and_factor",
    )(kernel)


def factor_slabs(fac):
    rows = lax.broadcasted_iota(jnp.int32, (8, 128), 0)
    for i in range(16):
        lo = 8 * i
        left = fac[lo : lo + 8, 0:128]
        right = fac[lo : lo + 8, 128:256]
        cols = [jnp.broadcast_to(left[:, lo + q : lo + q + 1], (8, 128)) for q in range(8)]
        for q in range(8):
            pivot = jnp.broadcast_to(cols[q][q : q + 1, :], (8, 128))
            inv = lax.rsqrt(pivot)
            coef = jnp.where(rows > q, cols[q] * inv, 0.0)
            scale = jnp.where(rows == q, inv, 1.0)
            u_left = jnp.broadcast_to(left[q : q + 1, :], (8, 128)) * inv
            u_right = jnp.broadcast_to(right[q : q + 1, :], (8, 128)) * inv
            left = left * scale - coef * u_left
            right = right * scale - coef * u_right
            for m in range(q + 1, 8):
                head = jnp.broadcast_to(cols[m][q : q + 1, :], (8, 128)) * inv
                cols[m] = cols[m] - coef * head
        fac[lo : lo + 8, 128:256] = right
        if i < 15:
            low = lo + 8
            wide = jnp.concatenate([left, right], axis=1)
            fac[low:128, :] = fac[low:128, :] - dot(left, wide, 0, 0)[low:128, :]


def factor(dd, pc, gl, mat, fac, col, panel_wait, send):
    ident = (
        lax.broadcasted_iota(jnp.int32, (128, 128), 0)
        == lax.broadcasted_iota(jnp.int32, (128, 128), 1)
    ).astype(F32)
    mat[...] = jnp.zeros_like(mat)
    for b in range(4):
        mat[b, :, 512 + 128 * b : 640 + 128 * b] = ident
    for q in range(2):
        mat[q, :, 0:256] = dd[0, 128 * q : 128 * q + 128, :]
        mat[q, :, 256:512] = dd[1, 128 * q : 128 * q + 128, :]
        mat[q + 2, :, 256:512] = dd[2, 128 * q : 128 * q + 128, :]

    def block(b, carry):
        fac[:, 0:128] = mat[b, :, pl.ds(pl.multiple_of(b * 128, 128), 128)]
        fac[:, 128:256] = ident
        factor_slabs(fac)
        panel = dot(fac[:, 128:256], mat[b])
        mat[b] = panel

        def trail(i, c2):
            lhs = mat[b, :, pl.ds(pl.multiple_of(i * 128, 128), 128)]
            mat[i] = mat[i] - dot(lhs, mat[b], 0, 0)
            return c2
        lax.fori_loop(b + 1, 4, trail, 0)
        return carry
    lax.fori_loop(0, 4, block, 0)

    wide = mat[...].reshape(512, 1024)
    winv = wide[:, 512:1024]
    tri = lax.broadcasted_iota(jnp.int32, (NB, NB), 0) >= lax.broadcasted_iota(jnp.int32, (NB, NB), 1)
    for h in range(2):
        own = slice(256 * h, 256 * h + 256)
        gl[512:768, own] = jnp.where(tri, wide[own, own].T, 0.0)
    send(2)
    panel_wait()
    solved = dot(winv[:, 0:256], pc[0], 1, 1) + dot(winv[:, 256:512], pc[1], 1, 1)
    for h in range(2):
        rows = slice(256 * h, 256 * h + 256)
        gl[rows, :] = dot(winv[:, rows], solved, 0, 0)
        for q in range(2):
            @pl.when(col == q)
            def _():
                gl[rows, 0:256] = -winv[256 * q : 256 * q + 256, rows].T
        send(h)


def update_kernel(a, rr, gl, out, hi, lo):
    row = lax.axis_index("row")
    col = lax.axis_index("col")
    slot = pl.program_id(0)

    @pl.when(slot == 0)
    def _():
        g = gl[0:512, :]
        top = g.astype(jnp.bfloat16)
        hi[...] = top
        lo[...] = (g - top.astype(F32)).astype(jnp.bfloat16)

    def mul(p, q):
        return jnp.dot(p, q, preferred_element_type=F32)

    acc = jnp.zeros((NB, 512), F32)
    for kk in range(2):
        r = rr[slot % 4, kk, pl.ds(pl.multiple_of(slot // 4 * NB, NB), NB), :]
        top = r.astype(jnp.bfloat16)
        rest = (r - top.astype(F32)).astype(jnp.bfloat16)
        rows = slice(kk * NB, kk * NB + NB)
        acc = acc + mul(top, hi[rows, :]) + (mul(top, lo[rows, :]) + mul(rest, hi[rows, :]))
    panel = (lax.broadcasted_iota(jnp.int32, (NB, 512), 1) < NB) & (col < 2)
    out[...] = jnp.where(panel, 0.0, a[...]) - acc

    @pl.when((slot == 0) & (row < 2))
    def _():
        out[:, 256:512] = jnp.zeros((NB, NB), F32)
        for q in range(2):
            @pl.when((row == q) & (col == q))
            def _():
                out[:, 0:256] = gl[512:768, 256 * q : 256 * q + 256]

        @pl.when((col > 1) | ((row == 0) & (col == 1)))
        def _():
            out[:, 0:256] = jnp.zeros((NB, NB), F32)


def update(kernel, rr, gl):
    vmem = pl.BlockSpec(memory_space=pltpu.VMEM)
    return pl.pallas_call(
        update_kernel,
        out_shape=jax.ShapeDtypeStruct(kernel.shape, F32),
        grid=(8,),
        in_specs=[pl.BlockSpec((NB, 512), lambda j: (j, 0)), vmem, vmem],
        out_specs=pl.BlockSpec((NB, 512), lambda j: (j, 0)),
        scratch_shapes=[pltpu.VMEM((512, 512), jnp.bfloat16)] * 2,
        compiler_params=pltpu.CompilerParams(vmem_limit_bytes=24 << 20),
        name="update_trailing",
    )(kernel, rr, gl)


def local(kernel):
    rr, gl = gather_and_factor(kernel)
    return update(kernel, rr, gl)


def solution(mesh):
    placed = (P("row", "col"),)
    return jax.shard_map(
        local, mesh=mesh, in_specs=placed, out_specs=P("row", "col"), check_vma=False
    )
```

time: 132 us -> 106 us (0.80)
  the two profiles are of different devices: /device:TPU:161 before, /device:TPU:181 now
where the time goes in v3:
time: 106 us
  Pallas kernels  102 us (96%)
  local copies, waits for them, and re-layouts  3.59 us (3%)
    pallas_call x1, Pallas kernels, gather_and_factor(): pl.pallas_call(main_kernel, out_shape=(jax.ShapeDtypeStruct((4, 2, 512, N...  96.1 us
    pallas_call x1, Pallas kernels, update(): pl.pallas_call(update_kernel, out_shape=jax.ShapeDtypeStruct(kernel.shape...  6.19 us
    unnamed x6, local copies, waits for them, and re-layouts  3.59 us

profile of v3, /device:TPU:181, one launch (start us, length us, event | category | flops | bytes accessed | tf_op | source)
XLA Modules:
  0.0 105.9 jit_solution(11369282181420199199)
XLA Ops:
  0.0 0.0 copy-start
  0.0 96.1 %gather_and_factor.1 = (f32[4,2,512,256]{3,2,1,0:T(8,128)}, f32[768,512]{1,0:T(8,128)}) custom-call(f32[2048,512]{1,0:T(8,128)} %a.3), custom_call_target="tpu_custom_call" | custom-call | tf_op jit(solution)/shard_map/gather_and_factor/pallas_call | solution.py:360
  96.1 0.0 copy-done
  96.1 0.0 copy-start.1
  96.1 2.2 %copy-done.1 = f32[4,2,512,256]{3,2,1,0:T(8,128)S(1)} copy-done((f32[4,2,512,256]{3,2,1,0:T(8,128)S(1)}, f32[4,2,512,256]{3,2,1,0:T(8,128)}, u32[]{:S(2)}) %copy-start.1) | copy-done | bytes 4194328
  98.3 0.0 copy-start.2
  98.3 1.4 %copy-done.2 = f32[768,512]{1,0:T(8,128)S(1)} copy-done((f32[768,512]{1,0:T(8,128)S(1)}, f32[768,512]{1,0:T(8,128)}, u32[]{:S(2)}) %copy-start.2) | copy-done | bytes 1572888
  99.7 6.2 %update_trailing.1 = f32[2048,512]{1,0:T(8,128)} custom-call(f32[2048,512]{1,0:T(8,128)S(1)} %copy-done, f32[4,2,512,256]{3,2,1,0:T(8,128)S(1)} %copy-done.1, f32[768,512]{1,0:T(8,128)S(1)} %copy-done.2), custom_call_target="tpu_custom_call" | custom-call | tf_op jit(solution)/shard_map/update_trailing/pallas_call | solution.py:511
Async XLA Ops:
  0.0 96.1 %copy-start = (f32[2048,512]{1,0:T(8,128)S(1)}, f32[2048,512]{1,0:T(8,128)}, u32[]{:S(2)}) copy-start(f32[2048,512]{1,0:T(8,128)} %a.3) | copy-start | bytes 12582916
  96.1 2.2 %copy-start.1 = (f32[4,2,512,256]{3,2,1,0:T(8,128)S(1)}, f32[4,2,512,256]{3,2,1,0:T(8,128)}, u32[]{:S(2)}) copy-start(f32[4,2,512,256]{3,2,1,0:T(8,128)} %get-tuple-element.7.rr) | copy-start | bytes 12582916
  98.3 1.4 %copy-start.2 = (f32[768,512]{1,0:T(8,128)S(1)}, f32[768,512]{1,0:T(8,128)}, u32[]{:S(2)}) copy-start(f32[768,512]{1,0:T(8,128)} %get-tuple-element.8.gl) | copy-start | bytes 4718596

commit v4 on v3

--- a/solution.py
+++ b/solution.py
@@ -10,12 +10,13 @@
 MESH = pl.DeviceIdType.MESH
 HI = lax.Precision.HIGHEST
 
+SLAB = 16
 CH = 64
 DH = 32
 PC_N = 512 // CH
 D_N = NB // DH
 LAGS = (0, 1, 2, 3)
-ZP, ZM, YP, YM, XP, XM, PA, CP, CM = range(9)
+ZP, ZM, YP, YM, XP, XM, PA, CP, CM, CF = range(10)
 
 
 def dot(a, b, ca=1, cb=0):
@@ -25,7 +26,7 @@
 
 
 def main_kernel(
-    a, rr, gl, pc, oth, dd, head, headt, mat, fac,
+    a, rr, gl, own_a, pc, oth, dd, headt, mat, fac,
     dsend, drecv, psend, precv, ppass, zsend, zrecv, ysend, yrecv,
     osend, orecv, gsend, grecv, lsem,
 ):
@@ -47,10 +48,11 @@
         PA: at(x, y, z, 1 - k),
         CP: at(x + 1, y, z, 1),
         CM: at(x + 3, y, z, 1),
+        CF: at(x + 2, y, z, 1),
     }
     barrier = pltpu.get_barrier_semaphore()
     for target in [near[way] for way in range(7)] + [
-        at(x + 1, y, z, 1 - k), at(x + 3, y, z, 1 - k)
+        at(x + 1, y, z, 1 - k), at(x + 3, y, z, 1 - k), at(x + 2, y, z, 0), at(x + 2, y, z, 1)
     ]:
         pl.semaphore_signal(barrier, inc=1, device_id=target, device_id_type=MESH)
 
@@ -60,20 +62,24 @@
             device_id=near[way], device_id_type=MESH,
         )
 
+    top = pltpu.make_async_copy(a.at[pl.ds(0, NB), :], own_a.at[pl.ds(0, NB), :], lsem.at[0])
+    top.start()
+    low_rows = pl.ds(NB, 2048 - NB)
+    bottom = pltpu.make_async_copy(a.at[low_rows, :], own_a.at[low_rows, :], lsem.at[4])
+    bottom.start()
+    top.wait()
+
     def rows_of(t, size):
         return pl.ds(pl.multiple_of(t * size, size), size)
 
     @pl.when(x == 0)
     def _():
-        load = pltpu.make_async_copy(a.at[pl.ds(0, NB), :], head, lsem.at[0])
-        load.start()
-        load.wait()
-        headt[...] = head[...].T
+        headt[...] = own_a[0:NB, :].T
 
     @pl.when((x == 0) & (y == 0) & (z < 2) & ((k == 0) | (z == 1)))
     def _():
         own = pltpu.make_async_copy(
-            a.at[pl.ds(0, NB), pl.ds(0, NB)], dd.at[z + k], lsem.at[1]
+            own_a.at[pl.ds(0, NB), pl.ds(0, NB)], dd.at[z + k], lsem.at[1]
         )
         own.start()
         own.wait()
@@ -108,7 +114,7 @@
     def d_whole(i, way):
         return remote(dd.at[i], dd.at[i], dsend.at[way, i], drecv.at[i, 0], way)
 
-    def d_block(i):
+    def d_block(i, begin, end):
         def one(t):
             if i == 2:
                 d_copy(i, t, PA).wait_recv()
@@ -121,7 +127,7 @@
                 @pl.when(goes)
                 def _():
                     d_copy(i, t, way).start()
-        loop(D_N, one)
+        loop(end, one, begin)
 
     def p_copy(kk, t, way):
         part = pc.at[kk, rows_of(t, CH), :]
@@ -146,10 +152,6 @@
 
     def p_step(kk, t):
         p_copy(kk, t, PA).wait_recv()
-
-        @pl.when(x == 1)
-        def _():
-            p_copy(kk, t, CP).start()
         p_pass(kk, t).start()
 
     held = (oth, rr)
@@ -223,7 +225,7 @@
 
     @pl.when(k == 1)
     def _carry():
-        pl.semaphore_wait(barrier, 9)
+        pl.semaphore_wait(barrier, 11)
 
         @pl.when(d_root[2])
         def _():
@@ -234,20 +236,25 @@
             fill_own(1).start()
 
             def first(t):
-                for way in (CP, CM, PA):
+                for way in (CP, CM, CF, PA):
                     p_first(1, t, way).start()
             loop(PC_N, first)
             fill_own(1).wait()
 
         def stage0(t):
+            early = source[0] | source[1]
+            first = jnp.where(early, 0, PC_N // 2)
+
+            @pl.when((x > 0) & (t >= first) & (t < first + PC_N // 2))
+            def _():
+                for q in range(2):
+                    for kk in range(2):
+                        p_step(kk, 2 * (t - first) + q)
+
+            @pl.when(x == 0)
+            def _():
+                p_copy(0, t, PA).wait_recv()
             for kk in range(2):
-                @pl.when(x > 0)
-                def _():
-                    p_step(kk, t)
-                if kk == 0:
-                    @pl.when(x == 0)
-                    def _():
-                        p_copy(0, t, PA).wait_recv()
                 for g in range(2):
                     @pl.when(source[g])
                     def _():
@@ -296,15 +303,12 @@
 
         @pl.when(x == 0)
         def _():
-            for way in (CP, CM, PA):
+            for way in (CP, CM, CF, PA):
                 p_whole(1, way).wait_send()
 
         @pl.when(x > 0)
         def _():
             for kk in range(2):
-                @pl.when(x == 1)
-                def _():
-                    p_whole(kk, CP).wait_send()
                 p_whole(kk, PA).wait_send()
 
         @pl.when(d_root[2])
@@ -315,17 +319,28 @@
 
     @pl.when(k == 0)
     def _factor():
-        pl.semaphore_wait(barrier, 9)
+        ident = (
+            lax.broadcasted_iota(jnp.int32, (128, 128), 0)
+            == lax.broadcasted_iota(jnp.int32, (128, 128), 1)
+        ).astype(F32)
+        mat[...] = jnp.zeros_like(mat)
+        for b in range(4):
+            mat[b, :, 512 + 128 * b : 640 + 128 * b] = ident
+        pl.semaphore_wait(barrier, 11)
 
         @pl.when(x == 0)
         def _():
             def first(t):
-                for way in (PA, CP, CM):
+                for way in (PA, CP, CM, CF):
                     p_first(0, t, way).start()
             loop(PC_N, first)
             fill_own(0).start()
-        for i in range(3):
-            d_block(i)
+        d_block(0, 0, D_N // 2)
+
+        def d_rest():
+            d_block(0, D_N // 2, D_N)
+            d_block(1, 0, D_N)
+            d_block(2, 0, D_N)
 
         def panel_wait():
             @pl.when(x == 0)
@@ -337,7 +352,7 @@
                 p_whole(0, PA).wait_recv()
             p_whole(1, PA).wait_recv()
 
-        factor(dd, pc, gl, mat, fac, col, panel_wait, lambda h: g_copy(h).start())
+        factor(dd, pc, gl, mat, fac, col, d_rest, panel_wait, lambda h: g_copy(h).start())
 
         remote(oth, rr, osend.at[0], orecv.at[0], PA).wait_recv()
         for i in range(3):
@@ -348,10 +363,12 @@
 
         @pl.when(x == 0)
         def _():
-            for way in (PA, CP, CM):
+            for way in (PA, CP, CM, CF):
                 p_whole(0, way).wait_send()
         for h in range(3):
             g_copy(h).wait_send()
+
+    bottom.wait()
 
 
 def gather_and_factor(kernel):
@@ -362,20 +379,20 @@
         out_shape=(
             jax.ShapeDtypeStruct((4, 2, 512, NB), F32),
             jax.ShapeDtypeStruct((768, 512), F32),
+            jax.ShapeDtypeStruct((2048, 512), F32),
         ),
         in_specs=[pl.BlockSpec(memory_space=pltpu.HBM)],
-        out_specs=(vmem, vmem),
+        out_specs=(vmem, vmem, vmem),
         scratch_shapes=[
             pltpu.VMEM((2, 512, NB), F32),
             pltpu.VMEM((4, 2, 512, NB), F32),
             pltpu.VMEM((3, NB, NB), F32),
-            pltpu.VMEM((NB, 512), F32),
             pltpu.VMEM((512, NB), F32),
             pltpu.VMEM((4, 128, 1024), F32),
             pltpu.VMEM((128, 256), F32),
             dma((7, 3)),
             dma((3, D_N)),
-            dma((3, 2)),
+            dma((4, 2)),
             dma((2, PC_N)),
             dma((2,)),
             dma((2, 2)),
@@ -386,10 +403,10 @@
             dma((1,)),
             dma((3,)),
             dma((3,)),
-            dma((4,)),
+            dma((5,)),
         ],
         compiler_params=pltpu.CompilerParams(
-            collective_id=0, has_side_effects=True, vmem_limit_bytes=56 << 20
+            collective_id=0, has_side_effects=True, vmem_limit_bytes=44 << 20
         ),
         name="gather_and_factor",
     )(kernel)
@@ -397,75 +414,124 @@
 
 def factor_slabs(fac):
     rows = lax.broadcasted_iota(jnp.int32, (8, 128), 0)
-    for i in range(16):
-        lo = 8 * i
-        left = fac[lo : lo + 8, 0:128]
-        right = fac[lo : lo + 8, 128:256]
-        cols = [jnp.broadcast_to(left[:, lo + q : lo + q + 1], (8, 128)) for q in range(8)]
-        for q in range(8):
-            pivot = jnp.broadcast_to(cols[q][q : q + 1, :], (8, 128))
-            inv = lax.rsqrt(pivot)
-            coef = jnp.where(rows > q, cols[q] * inv, 0.0)
-            scale = jnp.where(rows == q, inv, 1.0)
-            u_left = jnp.broadcast_to(left[q : q + 1, :], (8, 128)) * inv
-            u_right = jnp.broadcast_to(right[q : q + 1, :], (8, 128)) * inv
-            left = left * scale - coef * u_left
-            right = right * scale - coef * u_right
-            for m in range(q + 1, 8):
-                head = jnp.broadcast_to(cols[m][q : q + 1, :], (8, 128)) * inv
-                cols[m] = cols[m] - coef * head
-        fac[lo : lo + 8, 128:256] = right
-        if i < 15:
-            low = lo + 8
-            wide = jnp.concatenate([left, right], axis=1)
-            fac[low:128, :] = fac[low:128, :] - dot(left, wide, 0, 0)[low:128, :]
-
-
-def factor(dd, pc, gl, mat, fac, col, panel_wait, send):
+
+    def spread(tile, r):
+        return jnp.broadcast_to(tile[r : r + 1, :], (8, 128))
+
+    for i in range(128 // SLAB):
+        lo = SLAB * i
+        tiles = range(SLAB // 8)
+        left = [fac[lo + 8 * t : lo + 8 * t + 8, 0:128] for t in tiles]
+        right = [fac[lo + 8 * t : lo + 8 * t + 8, 128:256] for t in tiles]
+        cols = [
+            [jnp.broadcast_to(left[t][:, lo + q : lo + q + 1], (8, 128)) for t in tiles]
+            for q in range(SLAB)
+        ]
+        for q in range(SLAB):
+            tq, rq = q // 8, q % 8
+            inv = lax.rsqrt(spread(cols[q][tq], rq))
+            u_left = spread(left[tq], rq) * inv
+            u_right = spread(right[tq], rq) * inv
+            heads = {m: spread(cols[m][tq], rq) * inv for m in range(q + 1, SLAB)}
+            for t in range(tq, SLAB // 8):
+                coef = cols[q][t] * inv
+                if t == tq:
+                    coef = jnp.where(rows > rq, coef, 0.0)
+                    scale = jnp.where(rows == rq, inv, 1.0)
+                    left[t] = left[t] * scale
+                    right[t] = right[t] * scale
+                left[t] = left[t] - coef * u_left
+                right[t] = right[t] - coef * u_right
+                for m, head in heads.items():
+                    cols[m][t] = cols[m][t] - coef * head
+        for t in tiles:
+            fac[lo + 8 * t : lo + 8 * t + 8, 0:128] = left[t]
+            fac[lo + 8 * t : lo + 8 * t + 8, 128:256] = right[t]
+        low = lo + SLAB
+        if low < 128:
+            upper = jnp.concatenate(left, axis=0)
+            wide = jnp.concatenate([upper, jnp.concatenate(right, axis=0)], axis=1)
+            end = min(low + SLAB, 128)
+            fac[low:end, :] = fac[low:end, :] - dot(upper[:, low:end], wide, 0, 0)
+            if end < 128:
+                fac[end:128, :] = fac[end:128, :] - dot(upper[:, end:128], wide, 0, 0)
+
+
+def split(v):
+    top = v.astype(jnp.bfloat16)
+    return top, (v - top.astype(F32)).astype(jnp.bfloat16)
+
+
+def dot3(p, q, ca, cb):
+    def one(u, v):
+        return lax.dot_general(u, v, (((ca,), (cb,)), ((), ())), preferred_element_type=F32)
+    return one(p[0], q[0]) + (one(p[0], q[1]) + one(p[1], q[0]))
+
+
+def factor(dd, pc, gl, mat, fac, col, d_rest, panel_wait, send):
     ident = (
         lax.broadcasted_iota(jnp.int32, (128, 128), 0)
         == lax.broadcasted_iota(jnp.int32, (128, 128), 1)
     ).astype(F32)
-    mat[...] = jnp.zeros_like(mat)
-    for b in range(4):
-        mat[b, :, 512 + 128 * b : 640 + 128 * b] = ident
-    for q in range(2):
-        mat[q, :, 0:256] = dd[0, 128 * q : 128 * q + 128, :]
-        mat[q, :, 256:512] = dd[1, 128 * q : 128 * q + 128, :]
-        mat[q + 2, :, 256:512] = dd[2, 128 * q : 128 * q + 128, :]
+    mat[0, :, 0:256] = dd[0, 0:128, :]
 
     def block(b, carry):
-        fac[:, 0:128] = mat[b, :, pl.ds(pl.multiple_of(b * 128, 128), 128)]
+        here = pl.ds(pl.multiple_of(b * 128, 128), 128)
+        window = pl.ds(pl.multiple_of(b * 128 + 128, 128), 512)
+        fac[:, 0:128] = mat[b, :, here]
         fac[:, 128:256] = ident
         factor_slabs(fac)
-        panel = dot(fac[:, 128:256], mat[b])
-        mat[b] = panel
+        mat[b, :, here] = fac[:, 0:128]
+
+        @pl.when(b == 0)
+        def _():
+            d_rest()
+            mat[1, :, 0:256] = dd[0, 128:256, :]
+            for q in range(2):
+                mat[q, :, 256:512] = dd[1, 128 * q : 128 * q + 128, :]
+                mat[q + 2, :, 256:512] = dd[2, 128 * q : 128 * q + 128, :]
+        panel = dot(fac[:, 128:256], mat[b, :, window])
+        mat[b, :, window] = panel
 
         def trail(i, c2):
             lhs = mat[b, :, pl.ds(pl.multiple_of(i * 128, 128), 128)]
-            mat[i] = mat[i] - dot(lhs, mat[b], 0, 0)
+            mat[i, :, window] = mat[i, :, window] - dot(lhs, mat[b, :, window], 0, 0)
             return c2
         lax.fori_loop(b + 1, 4, trail, 0)
         return carry
     lax.fori_loop(0, 4, block, 0)
 
-    wide = mat[...].reshape(512, 1024)
-    winv = wide[:, 512:1024]
+    def winv(p, q):
+        return mat[2 * p : 2 * p + 2, :, 512 + 256 * q : 768 + 256 * q].reshape(NB, NB)
+
+    panel_wait()
+    w = {pq: split(winv(*pq)) for pq in ((0, 0), (1, 0), (1, 1))}
+    cols = [split(pc[q]) for q in range(2)]
+    one = split(dot3(w[0, 0], cols[0], 1, 1))
+    two = split(dot3(w[1, 0], cols[0], 1, 1) + dot3(w[1, 1], cols[1], 1, 1))
+
+    def own(h, q):
+        @pl.when(col == q)
+        def _():
+            gl[256 * h : 256 * h + 256, 0:256] = -winv(q, h).T
+
+    gl[256:512, :] = dot3(w[1, 1], two, 0, 0)
+    own(1, 0)
+    own(1, 1)
+    send(1)
+    gl[0:256, :] = dot3(w[0, 0], one, 0, 0) + dot3(w[1, 0], two, 0, 0)
+    own(0, 0)
+    own(0, 1)
+    send(0)
     tri = lax.broadcasted_iota(jnp.int32, (NB, NB), 0) >= lax.broadcasted_iota(jnp.int32, (NB, NB), 1)
-    for h in range(2):
-        own = slice(256 * h, 256 * h + 256)
-        gl[512:768, own] = jnp.where(tri, wide[own, own].T, 0.0)
+
+    @pl.when(col < 2)
+    def _():
+        for h in range(2):
+            span = slice(256 * h, 256 * h + 256)
+            upper = mat[2 * h : 2 * h + 2, :, span].reshape(NB, NB)
+            gl[512:768, span] = jnp.where(tri, upper.T, 0.0)
     send(2)
-    panel_wait()
-    solved = dot(winv[:, 0:256], pc[0], 1, 1) + dot(winv[:, 256:512], pc[1], 1, 1)
-    for h in range(2):
-        rows = slice(256 * h, 256 * h + 256)
-        gl[rows, :] = dot(winv[:, rows], solved, 0, 0)
-        for q in range(2):
-            @pl.when(col == q)
-            def _():
-                gl[rows, 0:256] = -winv[256 * q : 256 * q + 256, rows].T
-        send(h)
 
 
 def update_kernel(a, rr, gl, out, hi, lo):
@@ -491,7 +557,8 @@
         rows = slice(kk * NB, kk * NB + NB)
         acc = acc + mul(top, hi[rows, :]) + (mul(top, lo[rows, :]) + mul(rest, hi[rows, :]))
     panel = (lax.broadcasted_iota(jnp.int32, (NB, 512), 1) < NB) & (col < 2)
-    out[...] = jnp.where(panel, 0.0, a[...]) - acc
+    mine = a[pl.ds(pl.multiple_of(slot * NB, NB), NB), :]
+    out[...] = jnp.where(panel, 0.0, mine) - acc
 
     @pl.when((slot == 0) & (row < 2))
     def _():
@@ -512,7 +579,7 @@
         update_kernel,
         out_shape=jax.ShapeDtypeStruct(kernel.shape, F32),
         grid=(8,),
-        in_specs=[pl.BlockSpec((NB, 512), lambda j: (j, 0)), vmem, vmem],
+        in_specs=[vmem, vmem, vmem],
         out_specs=pl.BlockSpec((NB, 512), lambda j: (j, 0)),
         scratch_shapes=[pltpu.VMEM((512, 512), jnp.bfloat16)] * 2,
         compiler_params=pltpu.CompilerParams(vmem_limit_bytes=24 << 20),
@@ -521,8 +588,8 @@
 
 
 def local(kernel):
-    rr, gl = gather_and_factor(kernel)
-    return update(kernel, rr, gl)
+    rr, gl, own = gather_and_factor(kernel)
+    return update(own, rr, gl)
 
 
 def solution(mesh):

time: 106 us -> 82.4 us (0.78)
  the two profiles are of different devices: /device:TPU:181 before, /device:TPU:37 now
where the time goes in v4:
time: 82.4 us
  Pallas kernels  82.3 us (100%)
    pallas_call x1, Pallas kernels, gather_and_factor(): pl.pallas_call(main_kernel, out_shape=(jax.ShapeDtypeStruct((4, 2, 512, N...  76.1 us
    pallas_call x1, Pallas kernels, update(): pl.pallas_call(update_kernel, out_shape=jax.ShapeDtypeStruct(kernel.shape...  6.23 us

profile of v4, /device:TPU:37, one launch (start us, length us, event | category | flops | bytes accessed | tf_op | source)
XLA Modules:
  0.0 82.4 jit_solution(13090542455758160073)
XLA Ops:
  0.0 76.1 %gather_and_factor.1 = (f32[4,2,512,256]{3,2,1,0:T(8,128)S(1)}, f32[768,512]{1,0:T(8,128)S(1)}, f32[2048,512]{1,0:T(8,128)S(1)}) custom-call(f32[2048,512]{1,0:T(8,128)} %a.1), custom_call_target="tpu_custom_call" | custom-call | tf_op jit(solution)/shard_map/gather_and_factor/pallas_call | solution.py:377
  76.1 6.2 %update_trailing.1 = f32[2048,512]{1,0:T(8,128)} custom-call(f32[2048,512]{1,0:T(8,128)S(1)} %get-tuple-element.8.a, f32[4,2,512,256]{3,2,1,0:T(8,128)S(1)} %get-tuple-element.9.rr, f32[768,512]{1,0:T(8,128)S(1)} %get-tuple-element.10.gl), custom_call_target="tpu_custom_call" | custom-call | tf_op jit(solution)/shard_map/update_trailing/pallas_call | solution.py:578

commit v5 on v4

--- a/solution.py
+++ b/solution.py
@@ -16,7 +16,7 @@
 PC_N = 512 // CH
 D_N = NB // DH
 LAGS = (0, 1, 2, 3)
-ZP, ZM, YP, YM, XP, XM, PA, CP, CM, CF = range(10)
+ZP, ZM, YP, YM, Z2, Z6, Y2, PA, CP, CM, CF = range(11)
 
 
 def dot(a, b, ca=1, cb=0):
@@ -26,7 +26,7 @@
 
 
 def main_kernel(
-    a, rr, gl, own_a, pc, oth, dd, headt, mat, fac,
+    a, rr, gl, own_a, pc, oth, dd, headt, wb, ub, fac,
     dsend, drecv, psend, precv, ppass, zsend, zrecv, ysend, yrecv,
     osend, orecv, gsend, grecv, lsem,
 ):
@@ -38,22 +38,24 @@
     def at(nx, ny, nz, nk):
         return ((nx % 4) * 2 + nk, (ny % 4) * 8 + nz % 8)
 
+    urgent = jnp.where(z < 2, 1, z // 2)
     near = {
         ZP: at(x, y, z + 1, k),
         ZM: at(x, y, z + 7, k),
         YP: at(x, y + 1, z, k),
         YM: at(x, y + 3, z, k),
-        XP: at(x + 1, y, z, k),
-        XM: at(x + 3, y, z, k),
+        Z2: at(x, y, z + 2, k),
+        Z6: at(x, y, z + 6, k),
+        Y2: at(x, y + 2, z, k),
         PA: at(x, y, z, 1 - k),
-        CP: at(x + 1, y, z, 1),
-        CM: at(x + 3, y, z, 1),
-        CF: at(x + 2, y, z, 1),
+        CP: at(urgent, y, z, 1),
+        CM: at(jnp.where(urgent == 1, 2, 1), y, z, 1),
+        CF: at(jnp.where(urgent == 3, 2, 3), y, z, 1),
     }
     barrier = pltpu.get_barrier_semaphore()
-    for target in [near[way] for way in range(7)] + [
-        at(x + 1, y, z, 1 - k), at(x + 3, y, z, 1 - k), at(x + 2, y, z, 0), at(x + 2, y, z, 1)
-    ]:
+    greeted = [near[way] for way in (ZP, ZM, YP, YM, Z2, Z6, Y2, PA)]
+    greeted += [at(x + q, y, z, kk) for q in (1, 2, 3) for kk in (0, 1)]
+    for target in greeted:
         pl.semaphore_signal(barrier, inc=1, device_id=target, device_id_type=MESH)
 
     def remote(src, dst, send, recv, way):
@@ -76,10 +78,10 @@
     def _():
         headt[...] = own_a[0:NB, :].T
 
-    @pl.when((x == 0) & (y == 0) & (z < 2) & ((k == 0) | (z == 1)))
+    @pl.when((x == 0) & (y == 0) & (z == 0) & (k == 0))
     def _():
         own = pltpu.make_async_copy(
-            own_a.at[pl.ds(0, NB), pl.ds(0, NB)], dd.at[z + k], lsem.at[1]
+            own_a.at[pl.ds(0, NB), pl.ds(0, NB)], dd.at[0], lsem.at[1]
         )
         own.start()
         own.wait()
@@ -94,18 +96,20 @@
 
     d_root, d_ways = [], []
     for i in range(3):
-        dz = (z + 8 - min(i, 1)) % 8
-        line = (x == 0) & (y == 0)
-        root = line & (dz == 0)
-        d_root.append(root)
-        d_ways.append((
-            (ZP, line & (dz <= 3)),
-            (ZM, line & ((dz == 0) | (dz >= 6))),
-            (YP, (x == 0) & (y <= 1)),
-            (YM, (x == 0) & (y == 0)),
-            (XP, x <= 1),
-            (XM, x == 0),
-        ))
+        dz = (z + 8 - i // 2) % 8
+        d_root.append((y == 0) & (dz == 0))
+        if i == 0:
+            round_y = ((YP, d_root[i]), (YM, d_root[i]), (Y2, d_root[i]))
+            along_z = (
+                (Z2, (dz == 0) | (dz == 2)),
+                (Z6, dz == 0),
+                (ZP, (dz == 0) | (dz == 2)),
+                (ZM, (dz == 0) | (dz == 6)),
+            )
+        else:
+            round_y = ((YP, d_root[i]), (YM, ((y == 0) | (y == 3)) & (dz == 0)))
+            along_z = ((ZP, dz <= 3), (ZM, (dz == 0) | (dz >= 6)))
+        d_ways.append(round_y + along_z)
 
     def d_copy(i, t, way):
         part = dd.at[i, rows_of(t, DH), :]
@@ -114,14 +118,20 @@
     def d_whole(i, way):
         return remote(dd.at[i], dd.at[i], dsend.at[way, i], drecv.at[i, 0], way)
 
+    def d_seed(i, kk, t):
+        return remote(
+            pc.at[kk, rows_of(t, DH), :], dd.at[i, rows_of(t, DH), :],
+            dsend.at[PA, i], drecv.at[i, t], PA,
+        )
+
     def d_block(i, begin, end):
         def one(t):
-            if i == 2:
-                d_copy(i, t, PA).wait_recv()
-            else:
-                @pl.when(jnp.logical_not(d_root[i]))
+            if i == 0:
+                @pl.when(jnp.logical_not(d_root[0] & (x == 0)))
                 def _():
                     d_copy(i, t, PA).wait_recv()
+            else:
+                d_copy(i, t, PA).wait_recv()
 
             for way, goes in d_ways[i]:
                 @pl.when(goes)
@@ -147,11 +157,36 @@
             psend.at[way - PA, kk], recv, way,
         )
 
+    def send_first(kk):
+        @pl.when(z < 2)
+        def _():
+            def every(t):
+                for way in (CP, CM, CF, PA):
+                    p_first(kk, t, way).start()
+            loop(PC_N, every)
+
+        @pl.when(z >= 2)
+        def _():
+            def one(t):
+                for way in (CP, PA):
+                    p_first(kk, t, way).start()
+            loop(PC_N, one)
+
+            def two(t):
+                for way in (CM, CF):
+                    p_first(kk, t, way).start()
+            loop(PC_N, two)
+
     def fill_own(kk):
         return pltpu.make_async_copy(headt, pc.at[kk], lsem.at[2])
 
     def p_step(kk, t):
         p_copy(kk, t, PA).wait_recv()
+        for i in ((0,), (1, 2))[kk]:
+            @pl.when(d_root[i] & (t < NB // CH))
+            def _():
+                for q in range(CH // DH):
+                    d_seed(i, kk, CH // DH * t + q).start()
         p_pass(kk, t).start()
 
     held = (oth, rr)
@@ -225,24 +260,20 @@
 
     @pl.when(k == 1)
     def _carry():
-        pl.semaphore_wait(barrier, 11)
-
-        @pl.when(d_root[2])
-        def _():
-            loop(D_N, lambda t: d_copy(2, t, PA).start())
+        pl.semaphore_wait(barrier, 14)
 
         @pl.when(x == 0)
         def _():
+            send_first(1)
             fill_own(1).start()
-
-            def first(t):
-                for way in (CP, CM, CF, PA):
-                    p_first(1, t, way).start()
-            loop(PC_N, first)
             fill_own(1).wait()
+            for i in (1, 2):
+                @pl.when(d_root[i])
+                def _():
+                    loop(D_N, lambda t: d_seed(i, 1, t).start())
 
         def stage0(t):
-            early = source[0] | source[1]
+            early = source[0] | source[1] | d_root[0] | d_root[2]
             first = jnp.where(early, 0, PC_N // 2)
 
             @pl.when((x > 0) & (t >= first) & (t < first + PC_N // 2))
@@ -311,36 +342,34 @@
             for kk in range(2):
                 p_whole(kk, PA).wait_send()
 
-        @pl.when(d_root[2])
-        def _():
-            d_whole(2, PA).wait_send()
+        for i in range(3):
+            seeds = d_root[i] & (x > 0) if i == 0 else d_root[i]
+
+            @pl.when(seeds)
+            def _():
+                d_whole(i, PA).wait_send()
         for h in range(3):
             g_copy(h).wait_recv()
 
     @pl.when(k == 0)
     def _factor():
-        ident = (
-            lax.broadcasted_iota(jnp.int32, (128, 128), 0)
-            == lax.broadcasted_iota(jnp.int32, (128, 128), 1)
-        ).astype(F32)
-        mat[...] = jnp.zeros_like(mat)
-        for b in range(4):
-            mat[b, :, 512 + 128 * b : 640 + 128 * b] = ident
-        pl.semaphore_wait(barrier, 11)
+        pl.semaphore_wait(barrier, 14)
 
         @pl.when(x == 0)
         def _():
-            def first(t):
-                for way in (PA, CP, CM, CF):
-                    p_first(0, t, way).start()
-            loop(PC_N, first)
+            send_first(0)
             fill_own(0).start()
         d_block(0, 0, D_N // 2)
 
-        def d_rest():
-            d_block(0, D_N // 2, D_N)
-            d_block(1, 0, D_N)
-            d_block(2, 0, D_N)
+        def d_more(b, j):
+            q = D_N // 4
+            if b == 0:
+                if j < 2:
+                    d_block(0, (2 + j) * q, (3 + j) * q)
+                else:
+                    d_block(1, (j - 2) * 2 * q, (j - 1) * 2 * q)
+            else:
+                d_block(2, j * q, (j + 1) * q)
 
         def panel_wait():
             @pl.when(x == 0)
@@ -352,7 +381,7 @@
                 p_whole(0, PA).wait_recv()
             p_whole(1, PA).wait_recv()
 
-        factor(dd, pc, gl, mat, fac, col, d_rest, panel_wait, lambda h: g_copy(h).start())
+        factor(dd, pc, gl, wb, ub, fac, col, d_more, panel_wait, lambda h: g_copy(h).start())
 
         remote(oth, rr, osend.at[0], orecv.at[0], PA).wait_recv()
         for i in range(3):
@@ -388,9 +417,10 @@
             pltpu.VMEM((4, 2, 512, NB), F32),
             pltpu.VMEM((3, NB, NB), F32),
             pltpu.VMEM((512, NB), F32),
-            pltpu.VMEM((4, 128, 1024), F32),
+            pltpu.VMEM((2, NB, NB), F32),
+            pltpu.VMEM((2, NB, NB), F32),
             pltpu.VMEM((128, 256), F32),
-            dma((7, 3)),
+            dma((8, 3)),
             dma((3, D_N)),
             dma((4, 2)),
             dma((2, PC_N)),
@@ -412,7 +442,7 @@
     )(kernel)
 
 
-def factor_slabs(fac):
+def factor_slabs(fac, between):
     rows = lax.broadcasted_iota(jnp.int32, (8, 128), 0)
 
     def spread(tile, r):
@@ -448,6 +478,8 @@
             fac[lo + 8 * t : lo + 8 * t + 8, 0:128] = left[t]
             fac[lo + 8 * t : lo + 8 * t + 8, 128:256] = right[t]
         low = lo + SLAB
+        if i % 2 == 1:
+            between(i // 2)
         if low < 128:
             upper = jnp.concatenate(left, axis=0)
             wide = jnp.concatenate([upper, jnp.concatenate(right, axis=0)], axis=1)
@@ -468,69 +500,77 @@
     return one(p[0], q[0]) + (one(p[0], q[1]) + one(p[1], q[0]))
 
 
-def factor(dd, pc, gl, mat, fac, col, d_rest, panel_wait, send):
+def factor(dd, pc, gl, wb, ub, fac, col, d_more, panel_wait, send):
     ident = (
         lax.broadcasted_iota(jnp.int32, (128, 128), 0)
         == lax.broadcasted_iota(jnp.int32, (128, 128), 1)
     ).astype(F32)
-    mat[0, :, 0:256] = dd[0, 0:128, :]
-
-    def block(b, carry):
-        here = pl.ds(pl.multiple_of(b * 128, 128), 128)
-        window = pl.ds(pl.multiple_of(b * 128 + 128, 128), 512)
-        fac[:, 0:128] = mat[b, :, here]
+
+    def half(h, src, between, middle):
+        lo, hi = slice(0, 128), slice(128, 256)
+        fac[:, 0:128] = src[lo, lo]
         fac[:, 128:256] = ident
-        factor_slabs(fac)
-        mat[b, :, here] = fac[:, 0:128]
-
-        @pl.when(b == 0)
-        def _():
-            d_rest()
-            mat[1, :, 0:256] = dd[0, 128:256, :]
-            for q in range(2):
-                mat[q, :, 256:512] = dd[1, 128 * q : 128 * q + 128, :]
-                mat[q + 2, :, 256:512] = dd[2, 128 * q : 128 * q + 128, :]
-        panel = dot(fac[:, 128:256], mat[b, :, window])
-        mat[b, :, window] = panel
-
-        def trail(i, c2):
-            lhs = mat[b, :, pl.ds(pl.multiple_of(i * 128, 128), 128)]
-            mat[i, :, window] = mat[i, :, window] - dot(lhs, mat[b, :, window], 0, 0)
-            return c2
-        lax.fori_loop(b + 1, 4, trail, 0)
-        return carry
-    lax.fori_loop(0, 4, block, 0)
-
-    def winv(p, q):
-        return mat[2 * p : 2 * p + 2, :, 512 + 256 * q : 768 + 256 * q].reshape(NB, NB)
-
-    panel_wait()
-    w = {pq: split(winv(*pq)) for pq in ((0, 0), (1, 0), (1, 1))}
-    cols = [split(pc[q]) for q in range(2)]
-    one = split(dot3(w[0, 0], cols[0], 1, 1))
-    two = split(dot3(w[1, 0], cols[0], 1, 1) + dot3(w[1, 1], cols[1], 1, 1))
-
-    def own(h, q):
-        @pl.when(col == q)
-        def _():
-            gl[256 * h : 256 * h + 256, 0:256] = -winv(q, h).T
-
-    gl[256:512, :] = dot3(w[1, 1], two, 0, 0)
-    own(1, 0)
-    own(1, 1)
+        factor_slabs(fac, lambda j: between(0, j))
+        w0 = fac[:, 128:256]
+        wb[h, lo, lo] = w0
+        wb[h, lo, hi] = jnp.zeros((128, 128), F32)
+        ub[h, lo, lo] = fac[:, 0:128]
+        u01 = dot(w0, src[lo, hi])
+        ub[h, lo, hi] = u01
+        fac[:, 0:128] = src[hi, hi] - dot(u01, u01, 0, 0)
+        fac[:, 128:256] = ident
+        middle()
+        factor_slabs(fac, lambda j: between(1, j))
+        w1 = fac[:, 128:256]
+        ub[h, hi, hi] = fac[:, 0:128]
+        wb[h, hi, hi] = w1
+        wb[h, hi, lo] = -dot(w1, dot(u01, w0, 0, 0))
+
+    half(0, dd.at[0], d_more, lambda: None)
+    w_one = wb[0]
+    v = dot(w_one, dd[1])
+    ub[1] = dd[2] - dot(v, v, 0, 0)
+    w_one = split(w_one)
+    v = split(v)
+    kept = {}
+
+    def middle():
+        panel_wait()
+        one = dot3(w_one, split(pc[0]), 1, 1)
+        kept["one"] = dot3(w_one, split(one), 0, 0)
+        kept["two"] = pc[1].T - dot3(v, split(one), 0, 0)
+        kept["mix"] = split(dot3(w_one, v, 0, 0))
+
+    half(1, ub.at[1], lambda b, j: None, middle)
+    w_two = split(wb[1])
+    two = dot3(w_two, split(kept["two"]), 1, 0)
+    g_two = dot3(w_two, split(two), 0, 0)
+    gl[256:512, :] = g_two
+
+    @pl.when(col == 0)
+    def _():
+        gl[256:512, 0:256] = jnp.zeros((NB, NB), F32)
+
+    @pl.when(col == 1)
+    def _():
+        gl[256:512, 0:256] = -wb[1].T
     send(1)
-    gl[0:256, :] = dot3(w[0, 0], one, 0, 0) + dot3(w[1, 0], two, 0, 0)
-    own(0, 0)
-    own(0, 1)
+    gl[0:256, :] = kept["one"] - dot3(kept["mix"], split(g_two), 1, 0)
+
+    @pl.when(col == 0)
+    def _():
+        gl[0:256, 0:256] = -wb[0].T
+
+    @pl.when(col == 1)
+    def _():
+        gl[0:256, 0:256] = dot3(kept["mix"], w_two, 1, 1)
     send(0)
     tri = lax.broadcasted_iota(jnp.int32, (NB, NB), 0) >= lax.broadcasted_iota(jnp.int32, (NB, NB), 1)
 
     @pl.when(col < 2)
     def _():
         for h in range(2):
-            span = slice(256 * h, 256 * h + 256)
-            upper = mat[2 * h : 2 * h + 2, :, span].reshape(NB, NB)
-            gl[512:768, span] = jnp.where(tri, upper.T, 0.0)
+            gl[512:768, 256 * h : 256 * h + 256] = jnp.where(tri, ub[h].T, 0.0)
     send(2)
 
 

time: 82.4 us -> 78.1 us (0.948)
  the two profiles are of different devices: /device:TPU:37 before, /device:TPU:103 now
where the time goes in v5:
time: 78.1 us; the launch traced here: 78 us
  Pallas kernels  78 us (100%)
    pallas_call x1, Pallas kernels, gather_and_factor(): pl.pallas_call(main_kernel, out_shape=(jax.ShapeDtypeStruct((4, 2, 512, N...  71.7 us
    pallas_call x1, Pallas kernels, update(): pl.pallas_call(update_kernel, out_shape=jax.ShapeDtypeStruct(kernel.shape...  6.23 us

profile of v5, /device:TPU:103, one launch (start us, length us, event | category | flops | bytes accessed | tf_op | source)
XLA Modules:
  0.0 78.0 jit_solution(1575903032603762179)
XLA Ops:
  0.0 71.7 %gather_and_factor.1 = (f32[4,2,512,256]{3,2,1,0:T(8,128)S(1)}, f32[768,512]{1,0:T(8,128)S(1)}, f32[2048,512]{1,0:T(8,128)S(1)}) custom-call(f32[2048,512]{1,0:T(8,128)} %a.1), custom_call_target="tpu_custom_call" | custom-call | tf_op jit(solution)/shard_map/gather_and_factor/pallas_call | solution.py:406
  71.8 6.2 %update_trailing.1 = f32[2048,512]{1,0:T(8,128)} custom-call(f32[2048,512]{1,0:T(8,128)S(1)} %get-tuple-element.8.a, f32[4,2,512,256]{3,2,1,0:T(8,128)S(1)} %get-tuple-element.9.rr, f32[768,512]{1,0:T(8,128)S(1)} %get-tuple-element.10.gl), custom_call_target="tpu_custom_call" | custom-call | tf_op jit(solution)/shard_map/update_trailing/pallas_call | solution.py:618

commit v6 on v5

--- a/solution.py
+++ b/solution.py
@@ -100,12 +100,7 @@
         d_root.append((y == 0) & (dz == 0))
         if i == 0:
             round_y = ((YP, d_root[i]), (YM, d_root[i]), (Y2, d_root[i]))
-            along_z = (
-                (Z2, (dz == 0) | (dz == 2)),
-                (Z6, dz == 0),
-                (ZP, (dz == 0) | (dz == 2)),
-                (ZM, (dz == 0) | (dz == 6)),
-            )
+            along_z = ((ZP, dz <= 3), (ZM, (dz == 0) | (dz >= 6)))
         else:
             round_y = ((YP, d_root[i]), (YM, ((y == 0) | (y == 3)) & (dz == 0)))
             along_z = ((ZP, dz <= 3), (ZM, (dz == 0) | (dz >= 6)))
@@ -348,8 +343,12 @@
             @pl.when(seeds)
             def _():
                 d_whole(i, PA).wait_send()
-        for h in range(3):
+        for h in range(2):
             g_copy(h).wait_recv()
+
+        @pl.when(col < 2)
+        def _():
+            g_copy(2).wait_recv()
 
     @pl.when(k == 0)
     def _factor():
@@ -394,8 +393,12 @@
         def _():
             for way in (PA, CP, CM, CF):
                 p_whole(0, way).wait_send()
-        for h in range(3):
+        for h in range(2):
             g_copy(h).wait_send()
+
+        @pl.when(col < 2)
+        def _():
+            g_copy(2).wait_send()
 
     bottom.wait()
 
@@ -571,7 +574,7 @@
     def _():
         for h in range(2):
             gl[512:768, 256 * h : 256 * h + 256] = jnp.where(tri, ub[h].T, 0.0)
-    send(2)
+        send(2)
 
 
 def update_kernel(a, rr, gl, out, hi, lo):

time: 78.1 us -> 77.5 us (level)
  no operation moved by 1% of the time
where the time goes in v6:
time: 77.5 us; the launch traced here: 77.4 us
  Pallas kernels  77.4 us (100%)
    pallas_call x1, Pallas kernels, gather_and_factor(): pl.pallas_call(main_kernel, out_shape=(jax.ShapeDtypeStruct((4, 2, 512, N...  71.1 us
    pallas_call x1, Pallas kernels, update(): pl.pallas_call(update_kernel, out_shape=jax.ShapeDtypeStruct(kernel.shape...  6.23 us

profile of v6, /device:TPU:103, one launch (start us, length us, event | category | flops | bytes accessed | tf_op | source)
XLA Modules:
  0.0 77.4 jit_solution(1410274696229768251)
XLA Ops:
  0.0 71.1 %gather_and_factor.1 = (f32[4,2,512,256]{3,2,1,0:T(8,128)S(1)}, f32[768,512]{1,0:T(8,128)S(1)}, f32[2048,512]{1,0:T(8,128)S(1)}) custom-call(f32[2048,512]{1,0:T(8,128)} %a.1), custom_call_target="tpu_custom_call" | custom-call | tf_op jit(solution)/shard_map/gather_and_factor/pallas_call | solution.py:409
  71.2 6.2 %update_trailing.1 = f32[2048,512]{1,0:T(8,128)} custom-call(f32[2048,512]{1,0:T(8,128)S(1)} %get-tuple-element.8.a, f32[4,2,512,256]{3,2,1,0:T(8,128)S(1)} %get-tuple-element.9.rr, f32[768,512]{1,0:T(8,128)S(1)} %get-tuple-element.10.gl), custom_call_target="tpu_custom_call" | custom-call | tf_op jit(solution)/shard_map/update_trailing/pallas_call | solution.py:621
